TPU v7x, 512 devices: a whole 4x4x16 slice. The times are simulated.
512 devices in a mesh: gx: 64 (over y_lo, z, core), gy: 8 (over x, y_hi).
Axes of the slice: x: 4, y: 4 (y_hi: 2, y_lo: 2; y = y_hi * 2 + y_lo), z: 16, core: 2. Of those that a mesh axis runs over, the one named last changes fastest.
Arguments:
- dist: float32 [19, 8, 256, 1024], P(None, None, 'gx', 'gy'), as said below
- marker_cell: int32 [32768, 128], P(('gx', 'gy')), may hold values from 0 to 3583
- marker_side: int32 [32768, 128], P(('gx', 'gy')), may hold values 0 or 1
- marker_frac: float32 [32768, 128], P(('gx', 'gy')), may hold values from 0 to 1
- blade_vel: float32 [3, 32768, 128], P(None, ('gx', 'gy')), may hold values from -4 to 4
Outputs:
- new_dist: float32 [19, 8, 256, 1024], P(None, None, 'gx', 'gy')
- marker_force: float32 [3, 32768, 128], P(None, ('gx', 'gy'))
Inputs may be any that keep to these rules, and one draw needn't show every extreme that they name: `marker_cell`: a cell below the top plane of a tile. `dist`: every distribution is positive.
All inputs are finite; a program needn't handle non-finite values. No bound on the sum of `marker_side` on one device may be relied on, other than what follows from the above.
Results may differ from a plain program's by a relative error of at most 0.0003.
Values sent between devices are 32-bit elements; how exact they have to be, the bound alone decides.
A program may use at most 64 MiB of HBM per device.

v0:
```python
import jax
import jax.numpy as jnp
import numpy as np
from jax import lax
from jax.sharding import PartitionSpec as P

VELOCITIES = np.array(
    [
        [0, 0, 0],
        [1, 0, 0],
        [-1, 0, 0],
        [0, 1, 0],
        [0, -1, 0],
        [0, 0, 1],
        [0, 0, -1],
        [1, 1, 0],
        [-1, -1, 0],
        [1, -1, 0],
        [-1, 1, 0],
        [1, 0, 1],
        [-1, 0, -1],
        [1, 0, -1],
        [-1, 0, 1],
        [0, 1, 1],
        [0, -1, -1],
        [0, 1, -1],
        [0, -1, 1],
    ]
)
WEIGHTS = np.array([1.0 / 3.0] + [1.0 / 18.0] * 6 + [1.0 / 36.0] * 12)
EXPONENTS = [
    (0, 0, 0),
    (1, 0, 0),
    (0, 1, 0),
    (0, 0, 1),
    (2, 0, 0),
    (0, 2, 0),
    (0, 0, 2),
    (1, 1, 0),
    (0, 1, 1),
    (1, 0, 1),
    (2, 1, 0),
    (2, 0, 1),
    (1, 2, 0),
    (0, 2, 1),
    (1, 0, 2),
    (0, 1, 2),
    (2, 2, 0),
    (0, 2, 2),
    (2, 0, 2),
]
RATE_BY_ORDER = [0.0, 0.0, 1.6, 1.2, 1.4]
STIFFNESS = 2.0


def shifted_2(array, axis, by):
    peers = lax.axis_size(axis)
    return lax.ppermute(array, axis, [(i, (i + by) % peers) for i in range(peers)])


def extended(array, sides, width):
    for axis, dim in sides:
        peers, length = (lax.axis_size(axis), array.shape[dim])
        up = [(i, (i + 1) % peers) for i in range(peers)]
        down = [(j, i) for i, j in up]
        last = lax.slice_in_dim(array, length - width, length, axis=dim)
        initial = lax.slice_in_dim(array, 0, width, axis=dim)
        before = lax.ppermute(last, axis, up)
        after = lax.ppermute(initial, axis, down)
        array = jnp.concatenate([before, array, after], axis=dim)
    return array


def find_index(vector):
    return [position for position in range(19) if list(VELOCITIES[position]) == list(vector)][0]


def opposite_of(index):
    return find_index(-VELOCITIES[index])


def mirror_of(index):
    return find_index([VELOCITIES[index][0], VELOCITIES[index][1], -VELOCITIES[index][2]])


def invert_rows(rows):
    count = len(rows)
    work = [
        list(rows[row]) + [1.0 if col == row else 0.0 for col in range(count)]
        for row in range(count)
    ]
    for col in range(count):
        pivot = max(range(col, count), key=lambda row: abs(work[row][col]))
        work[col], work[pivot] = (work[pivot], work[col])
        scale = work[col][col]
        work[col] = [value / scale for value in work[col]]
        for row in range(count):
            if row != col:
                factor = work[row][col]
                work[row] = [value - factor * lead for value, lead in zip(work[row], work[col])]
    return [line[count:] for line in work]


def collision_table():
    moment_rows = [
        [
            float(vel[0]) ** expo[0] * float(vel[1]) ** expo[1] * float(vel[2]) ** expo[2]
            for vel in VELOCITIES
        ]
        for expo in EXPONENTS
    ]
    inverse = invert_rows(moment_rows)
    scaled = [
        [RATE_BY_ORDER[sum(EXPONENTS[row])] * value for value in moment_rows[row]]
        for row in range(19)
    ]
    table = [
        [sum((inverse[row][mid] * scaled[mid][col] for mid in range(19))) for col in range(19)]
        for row in range(19)
    ]
    return np.array(table, dtype=np.float32)


def fluid_moments(dist):
    density = jnp.sum(dist, axis=0)
    momentum = jnp.tensordot(
        jnp.asarray(VELOCITIES.T, jnp.float32), dist, axes=1, precision=lax.Precision.HIGHEST
    )
    return (density, momentum / density)


def collide(dist, density, velocity, force):
    table = jnp.asarray(VELOCITIES, jnp.float32)
    weights = jnp.asarray(WEIGHTS, jnp.float32).reshape(19, 1, 1, 1)
    along = jnp.tensordot(table, velocity, axes=1, precision=lax.Precision.HIGHEST)
    speed_sq = jnp.sum(velocity * velocity, axis=0)
    equil = weights * density * (1.0 + 3.0 * along + 4.5 * along * along - 1.5 * speed_sq)
    offeq = (dist - equil).reshape(19, -1)
    relaxed = jnp.dot(
        jnp.asarray(collision_table()), offeq, precision=lax.Precision.HIGHEST
    ).reshape(dist.shape)
    pushed = jnp.tensordot(table, force, axes=1, precision=lax.Precision.HIGHEST)
    return dist - relaxed + 3.0 * weights * pushed


def finish_planes(shifted, post):
    result = []
    for index in range(19):
        lift = int(VELOCITIES[index][2])
        moved = shifted[index]
        if lift == 1:
            moved = jnp.concatenate([post[opposite_of(index), :1], moved[:-1]], axis=0)
        elif lift == -1:
            moved = jnp.concatenate([moved[1:], shifted[mirror_of(index)][-1:]], axis=0)
        result.append(moved)
    return jnp.stack(result, axis=0)


def local(dist, marker_cell, marker_side, marker_frac, blade_vel):
    planes, tile_x, tile_y = (dist.shape[1], dist.shape[2], dist.shape[3])
    layer = tile_x * tile_y
    density, velocity = fluid_moments(dist)
    vel_flat = velocity.reshape(3, -1)
    cells = marker_cell.reshape(-1)
    faraway = marker_side.reshape(-1) == 1
    frac = marker_frac.reshape(-1)
    pushes_goal = blade_vel.reshape(3, -1)
    near_low = jnp.take(vel_flat, cells, axis=1)
    near_high = jnp.take(vel_flat, cells + layer, axis=1)
    empty = jnp.zeros((3, planes * layer), jnp.float32)
    sent_cells = jnp.where(faraway, cells, 0)
    got_cells = shifted_2(sent_cells, "gx", 1)
    answer = jnp.stack(
        [jnp.take(vel_flat, got_cells, axis=1), jnp.take(vel_flat, got_cells + layer, axis=1)],
        axis=0,
    )
    returned = shifted_2(answer, "gx", -1)
    lower = jnp.where(faraway, returned[0], near_low)
    upper = jnp.where(faraway, returned[1], near_high)
    marker_velocity = (1.0 - frac) * lower + frac * upper
    pushes = STIFFNESS * (pushes_goal - marker_velocity)
    low_part = (1.0 - frac) * pushes
    high_part = frac * pushes
    own_low = jnp.where(faraway, 0.0, low_part)
    own_high = jnp.where(faraway, 0.0, high_part)
    away = jnp.stack(
        [jnp.where(faraway, low_part, 0.0), jnp.where(faraway, high_part, 0.0)], axis=0
    )
    arrived = shifted_2(away, "gx", 1)
    force = empty.at[:, cells].add(own_low).at[:, cells + layer].add(own_high)
    force = force.at[:, got_cells].add(arrived[0]).at[:, got_cells + layer].add(arrived[1])
    force = force.reshape(3, planes, tile_x, tile_y)
    post = collide(dist, density, velocity, force)
    padded = extended(post, (("gx", 2), ("gy", 3)), 1)
    shifted = []
    for index in range(19):
        step_x = int(VELOCITIES[index][0])
        step_y = int(VELOCITIES[index][1])
        shifted.append(
            padded[index, :, 1 - step_x : 1 - step_x + tile_x, 1 - step_y : 1 - step_y + tile_y]
        )
    new_dist = finish_planes(shifted, post)
    return (new_dist, pushes.reshape(blade_vel.shape))


def solution(mesh):
    return jax.shard_map(
        local,
        mesh=mesh,
        in_specs=(
            P(None, None, "gx", "gy"),
            P(("gx", "gy"), None),
            P(("gx", "gy"), None),
            P(("gx", "gy"), None),
            P(None, ("gx", "gy"), None),
        ),
        out_specs=(P(None, None, "gx", "gy"), P(None, ("gx", "gy"), None)),
        check_vma=False,
    )
```

profile of v0, /device:TPU:1, one launch (start us, length us, event | category | flops | bytes accessed | tf_op | source)
XLA Modules:
  0.0 409.5 jit_solution(5869806637289345972)
XLA Ops:
  0.6 0.8 fusion.23
  1.5 4.9 %collective-permute-start = (s32[8192]{0:T(1024)S(1)}, s32[8192]{0:T(1024)S(1)}, u32[]{:S(2)}, u32[]{:S(2)}) collective-permute-start(s32[8192]{0:T(1024)S(1)} %get-tuple-element.62), channel_id=1, source_target_pairs={{0,8},{8,16},{16,24},{24,32},{32,40},{40,48},{48,56},{56,64},{64,7... | collective-permute-start | bytes 98312 | tf_op jit(solution)/shard_map/ppermute | solution.py:58
  6.4 0.8 compare_select_fusion
  7.3 1.0 reduce_sum.18
  8.3 1.5 multiply_reduce_fusion
  9.8 1.7 copy_subtract_fusion
  11.5 0.8 broadcast_multiply_fusion.1
  12.3 0.6 copy.122
  12.9 27.8 %gather_fusion.2 = f32[8192,3]{1,0:T(8,128)} fusion(f32[3,4096]{0,1:T(8,128)S(1)} %copy.122, s32[8192]{0:T(1024)S(1)} %get-tuple-element.60), kind=kCustom, calls=%fused_computation.2.clone | custom fusion | bytes 229376 | tf_op jit(solution)/shard_map/jit(_take)/gather | solution.py:168
  40.8 27.9 %gather_fusion.3 = f32[8192,3]{1,0:T(8,128)} fusion(f32[3,4096]{0,1:T(8,128)S(1)} %copy.122, s32[8192]{0:T(1024)S(1)} %get-tuple-element.61), kind=kCustom, calls=%fused_computation.3.clone | custom fusion | bytes 229376 | tf_op jit(solution)/shard_map/jit(_take)/gather | solution.py:169
  68.6 2.7 copy.121
  71.6 27.9 %gather_fusion = f32[8192,3]{1,0:T(8,128)} fusion(f32[3,4096]{0,1:T(8,128)S(1)} %copy.122, s32[8192]{0:T(1024)S(1)} %get-tuple-element.50), kind=kCustom, calls=%fused_computation.clone | custom fusion | bytes 229376 | tf_op jit(solution)/shard_map/jit(_take)/gather | solution.py:174
  99.4 27.8 %gather_fusion.1 = f32[8192,3]{1,0:T(8,128)} fusion(f32[3,4096]{0,1:T(8,128)S(1)} %copy.122, s32[8192]{0:T(1024)S(1)} %get-tuple-element.51), kind=kCustom, calls=%fused_computation.1.clone | custom fusion | bytes 229376 | tf_op jit(solution)/shard_map/jit(_take)/gather | solution.py:174
  127.3 7.6 %select_bitcast_fusion = (f32[1,3,8192]{1,2,0:T(8,128)}, f32[1,3,8192]{1,2,0:T(8,128)}) fusion(f32[8192,3]{1,0:T(8,128)} %gather_fusion.1, pred[8192]{0:T(1024)(128)(4,1)S(1)} %get-tuple-element.65, f32[8192,3]{1,0:T(8,128)} %gather_fusion, pred[8192]{0:T(1024)(128)(4,1)S(1)} %get-tuple-element.64), kind=kLoop, calls=%fused_computation.18 | loop fusion | flops 49152 | bytes 409600 | tf_op jit(solution)/shard_map/stack | solution.py:173
  134.9 2.9 copy.124
  137.8 2.9 copy.125
  140.7 0.2 pad_maximum_fusion.1
  140.8 5.8 %collective-permute-start.1 = (f32[2,3,8192]{2,0,1:T(2,128)S(1)}, f32[2,3,8192]{2,0,1:T(2,128)S(1)}, u32[]{:S(2)}, u32[]{:S(2)}) collective-permute-start(f32[2,3,8192]{2,0,1:T(2,128)S(1)} %pad_maximum_fusion.1), channel_id=1, source_target_pairs={{0,504},{8,0},{16,8},{24,16},{32,24},{40,32},{48,40},{56,48},{64,5... | collective-permute-start | bytes 589832 | tf_op jit(solution)/shard_map/ppermute | solution.py:58
  146.7 1.2 collective-permute-done.1
  148.0 2.6 copy.160
  150.6 2.6 copy.161
  153.2 11.3 %broadcast_multiply_fusion = (f32[3,8192]{0,1:T(8,128)}, f32[3,8192]{0,1:T(8,128)S(1)}) fusion(f32[8192,3]{1,0:T(8,128)} %gather_fusion.3, pred[8192]{0:T(1024)(128)(4,1)S(1)} %get-tuple-element.59, f32[1,3,8192]{1,2,0:T(8,128)} %copy.161, f32[8192]{0:T(1024)S(1)} %bitcast.195, f32[8192,3]{1,0:T(8,128)} %gather_fusion.2, ...), kind=kLoop, calls=%fused_computation.26 | loop fusion | flops 221184 | bytes 778240 | tf_op jit(solution)/shard_map/mul | solution.py:181
  164.6 7.6 %select_bitcast_fusion.3 = (f32[1,3,8192]{1,2,0:T(8,128)}, f32[1,3,8192]{1,2,0:T(8,128)}) fusion(f32[3,8192]{0,1:T(8,128)S(1)} %get-tuple-element.14, f32[8192]{0:T(1024)S(1)} %get-tuple-element.54, pred[8192]{0:T(1024)(128)(4,1)S(1)} %get-tuple-element.63, f32[8192]{0:T(1024)S(1)} %get-tuple-element.53), kind=kLoop, calls=%fused_computation.21 | loop fusion | flops 98304 | bytes 368640 | tf_op jit(solution)/shard_map/stack | solution.py:186
  172.2 2.9 copy.130
  175.0 2.9 copy.131
  178.1 1.9 collective-permute-start.2
  180.0 0.5 fusion.34
  180.5 0.2 reshape.121
  180.7 50.7 %scatter_custom_fusion = f32[3,4096]{0,1:T(8,128)S(1)} fusion(s32[8192]{0:T(1024)S(1)} %bitcast.198, f32[3,8192]{0,1:T(8,128)} %copy-done, f32[8192]{0:T(1024)S(1)} %get-tuple-element.54, f32[]{:T(128)} %constant.23.clone.1, pred[8192]{0:T(1024)(128)(4,1)S(1)} %get-tuple-element.63), kind=kCustom, calls=%fused_computation.10 | custom fusion | flops 73728 | bytes 4285440 | tf_op jit(solution)/shard_map/scatter-add | solution.py:190
  231.4 3.5 copy.154
  234.9 51.1 %scatter_custom_fusion.1 = f32[3,4096]{0,1:T(8,128)S(1)} fusion(f32[3,4096]{0,1:T(8,128)S(1)} %scatter_custom_fusion, s32[8192]{0:T(1024)S(1)} %bitcast.197, f32[3,8192]{0,1:T(8,128)} %copy-done, f32[8192]{0:T(1024)S(1)} %get-tuple-element.53, f32[]{:T(128)} %constant.23.clone.1, pred[8192]{0:T(1024)(128)(4,1)S(1)} %get-tuple-element.63), kind=kCustom, calls=%fused_computation.8 | custom fusion | flops 73728 | bytes 188420 | tf_op jit(solution)/shard_map/scatter-add | solution.py:190
  286.3 2.7 copy.132
  289.0 2.7 copy.133
  291.7 45.2 %scatter_fusion = f32[3,4096]{0,1:T(8,128)S(1)} fusion(f32[3,4096]{0,1:T(8,128)S(1)} %scatter_custom_fusion.1, s32[8192]{0:T(1024)S(1)} %get-tuple-element.52, f32[8192,3]{1,0:T(8,128)} %copy.132), kind=kCustom, calls=%fused_computation.6 | custom fusion | flops 24576 | bytes 327680 | tf_op jit(solution)/shard_map/scatter-add | solution.py:191
  336.9 45.2 %scatter_fusion.1 = f32[3,4096]{0,1:T(8,128)S(1)} fusion(f32[3,4096]{0,1:T(8,128)S(1)} %scatter_fusion, s32[8192]{0:T(1024)S(1)} %get-tuple-element.49, f32[8192,3]{1,0:T(8,128)} %copy.133), kind=kCustom, calls=%fused_computation.7 | custom fusion | flops 24576 | bytes 327680 | tf_op jit(solution)/shard_map/scatter-add | solution.py:191
  382.1 1.9 fusion.35
  384.1 0.2 bitcast_add_fusion
  384.3 3.9 collective-permute-start.3
  388.4 6.5 %collective-permute-start.4 = (f32[19,8,1,128]{3,1,2,0:T(8,128)S(1)}, f32[19,8,1,128]{3,1,2,0:T(8,128)S(1)}, u32[]{:S(2)}, u32[]{:S(2)}) collective-permute-start(f32[19,8,1,128]{3,1,2,0:T(8,128)S(1)} %get-tuple-element.43), channel_id=1, source_target_pairs={{8,0},{16,8},{24,16},{32,24},{40,32},{48,40},{56,48},{64,56},{72,6... | collective-permute-start | bytes 233480 | tf_op jit(solution)/shard_map/ppermute | solution.py:69
  395.0 0.8 collective-permute-done.4
  396.0 0.4 copy.138
  396.4 4.6 %collective-permute-start.5 = (f32[19,8,6,1]{0,1,3,2:T(8,128)S(1)}, f32[19,8,6,1]{0,1,3,2:T(8,128)S(1)}, u32[]{:S(2)}, u32[]{:S(2)}) collective-permute-start(f32[19,8,6,1]{0,1,3,2:T(8,128)S(1)} %copy.138), channel_id=1, source_target_pairs={{0,1},{1,2},{2,3},{3,4},{4,5},{5,6},{6,7},{7,0},{8,9},{9,10},{10,1... | collective-permute-start | bytes 10952 | tf_op jit(solution)/shard_map/ppermute | solution.py:68
  401.0 0.4 copy.140
  401.4 4.3 %collective-permute-start.6 = (f32[19,8,6,1]{0,1,3,2:T(8,128)S(1)}, f32[19,8,6,1]{0,1,3,2:T(8,128)S(1)}, u32[]{:S(2)}, u32[]{:S(2)}) collective-permute-start(f32[19,8,6,1]{0,1,3,2:T(8,128)S(1)} %copy.140), channel_id=1, source_target_pairs={{1,0},{2,1},{3,2},{4,3},{5,4},{6,5},{7,6},{0,7},{9,8},{10,9},{11,1... | collective-permute-start | bytes 10952 | tf_op jit(solution)/shard_map/ppermute | solution.py:69
  405.8 0.4 copy.139
  406.2 1.2 collective-permute-done.6
  407.4 0.4 copy.141
  408.7 0.8 copy.153
  (62 shorter events, 2.1 us)
Async XLA Ops:
  0.6 68.0 %copy-start.4 = (f32[3,64,128]{2,1,0:T(8,128)S(1)}, f32[3,64,128]{2,1,0:T(8,128)}, u32[]{:S(2)}) copy-start(f32[3,64,128]{2,1,0:T(8,128)} %param.15) | copy-start | bytes 294916
  1.5 70.0 %collective-permute-start = (s32[8192]{0:T(1024)S(1)}, s32[8192]{0:T(1024)S(1)}, u32[]{:S(2)}, u32[]{:S(2)}) collective-permute-start(s32[8192]{0:T(1024)S(1)} %get-tuple-element.62), channel_id=1, source_target_pairs={{0,8},{8,16},{16,24},{24,32},{32,40},{40,48},{48,56},{56,64},{64,7... | collective-permute-start | bytes 98312 | tf_op jit(solution)/shard_map/ppermute | solution.py:58
  134.9 11.7 %copy-start.2 = (s32[64,128]{1,0:T(8,128)S(1)}, s32[64,128]{1,0:T(8,128)}, u32[]{:S(2)}) copy-start(s32[64,128]{1,0:T(8,128)} %param.12) | copy-start | bytes 98308
  140.8 7.0 %collective-permute-start.1 = (f32[2,3,8192]{2,0,1:T(2,128)S(1)}, f32[2,3,8192]{2,0,1:T(2,128)S(1)}, u32[]{:S(2)}, u32[]{:S(2)}) collective-permute-start(f32[2,3,8192]{2,0,1:T(2,128)S(1)} %pad_maximum_fusion.1), channel_id=1, source_target_pairs={{0,504},{8,0},{16,8},{24,16},{32,24},{40,32},{48,40},{56,48},{64,5... | collective-permute-start | bytes 589832 | tf_op jit(solution)/shard_map/ppermute | solution.py:58
  148.0 5.3 %copy-start.3 = (f32[64,128]{1,0:T(8,128)S(1)}, f32[64,128]{1,0:T(8,128)}, u32[]{:S(2)}) copy-start(f32[64,128]{1,0:T(8,128)} %param.14) | copy-start | bytes 98308
  164.5 7.6 %copy-start = (f32[3,8192]{0,1:T(8,128)}, f32[3,8192]{0,1:T(8,128)S(1)}, u32[]{:S(2)}) copy-start(f32[3,8192]{0,1:T(8,128)S(1)} %get-tuple-element.14) | copy-start | bytes 294916
  172.2 7.8 %copy-start.5 = (f32[19,19]{1,0:T(8,128)S(1)}, f32[19,19]{1,0:T(8,128)}, u32[]{:S(2)}) copy-start(f32[19,19]{1,0:T(8,128)} %constant.48.clone) | copy-start | bytes 4336
  178.1 107.9 %collective-permute-start.2 = (f32[2,3,8192]{2,0,1:T(2,128)S(1)}, f32[2,3,8192]{2,0,1:T(2,128)S(1)}, u32[]{:S(2)}, u32[]{:S(2)}) collective-permute-start(f32[2,3,8192]{2,0,1:T(2,128)S(1)} %pad_maximum_fusion.2), channel_id=1, source_target_pairs={{0,8},{8,16},{16,24},{24,32},{32,40},{40,48},{48,56},{56,64},{64,7... | collective-permute-start | bytes 589832 | tf_op jit(solution)/shard_map/ppermute | solution.py:58
  289.0 93.1 %copy-start.6 = (f32[19,3,1,1]{0,1,3,2:T(4,128)S(1)}, f32[19,3,1,1]{0,1,3,2:T(4,128)}, u32[]{:S(2)}) copy-start(f32[19,3,1,1]{0,1,3,2:T(4,128)} %constant.55) | copy-start | bytes 688
  291.7 92.4 %copy-start.1 = (f32[19,8,4,128]{3,2,1,0:T(4,128)S(1)}, f32[19,8,4,128]{3,2,1,0:T(4,128)}, u32[]{:S(2)}) copy-start(f32[19,8,4,128]{3,2,1,0:T(4,128)} %param.11) | copy-start | bytes 933892
  291.7 92.4 %copy-start.7 = (f32[19]{0:T(128)S(1)}, f32[19]{0:T(128)}, u32[]{:S(2)}) copy-start(f32[19]{0:T(128)} %constant.54) | copy-start | bytes 232
  384.3 10.6 %collective-permute-start.3 = (f32[19,8,1,128]{3,1,2,0:T(8,128)S(1)}, f32[19,8,1,128]{3,1,2,0:T(8,128)S(1)}, u32[]{:S(2)}, u32[]{:S(2)}) collective-permute-start(f32[19,8,1,128]{3,1,2,0:T(8,128)S(1)} %get-tuple-element.44), channel_id=1, source_target_pairs={{0,8},{8,16},{16,24},{24,32},{32,40},{40,48},{48,56},{56,64},{64,7... | collective-permute-start | bytes 233480 | tf_op jit(solution)/shard_map/ppermute | solution.py:68
  388.4 7.4 %collective-permute-start.4 = (f32[19,8,1,128]{3,1,2,0:T(8,128)S(1)}, f32[19,8,1,128]{3,1,2,0:T(8,128)S(1)}, u32[]{:S(2)}, u32[]{:S(2)}) collective-permute-start(f32[19,8,1,128]{3,1,2,0:T(8,128)S(1)} %get-tuple-element.43), channel_id=1, source_target_pairs={{8,0},{16,8},{24,16},{32,24},{40,32},{48,40},{56,48},{64,56},{72,6... | collective-permute-start | bytes 233480 | tf_op jit(solution)/shard_map/ppermute | solution.py:69
  396.4 9.3 %collective-permute-start.5 = (f32[19,8,6,1]{0,1,3,2:T(8,128)S(1)}, f32[19,8,6,1]{0,1,3,2:T(8,128)S(1)}, u32[]{:S(2)}, u32[]{:S(2)}) collective-permute-start(f32[19,8,6,1]{0,1,3,2:T(8,128)S(1)} %copy.138), channel_id=1, source_target_pairs={{0,1},{1,2},{2,3},{3,4},{4,5},{5,6},{6,7},{7,0},{8,9},{9,10},{10,1... | collective-permute-start | bytes 10952 | tf_op jit(solution)/shard_map/ppermute | solution.py:68
  401.4 6.1 %collective-permute-start.6 = (f32[19,8,6,1]{0,1,3,2:T(8,128)S(1)}, f32[19,8,6,1]{0,1,3,2:T(8,128)S(1)}, u32[]{:S(2)}, u32[]{:S(2)}) collective-permute-start(f32[19,8,6,1]{0,1,3,2:T(8,128)S(1)} %copy.140), channel_id=1, source_target_pairs={{1,0},{2,1},{3,2},{4,3},{5,4},{6,5},{7,6},{0,7},{9,8},{10,9},{11,1... | collective-permute-start | bytes 10952 | tf_op jit(solution)/shard_map/ppermute | solution.py:69
where the time goes:
time: 415 us; the launch traced here: 409 us
  other arithmetic  224 us (54%)
  local copies, waits for them, and re-layouts  144 us (35%)
  starting transfers between devices  32 us (8%)
  matrix products  5.6 us (1%)
    scatter-add x2, other arithmetic, local(): force = empty.at[:, cells].add(own_low).at[:, cells + layer].add(own_high)  102 us
    scatter-add x2, other arithmetic, local(): force.at[:, got_cells].add(arrived[0]).at[:, got_cells + layer]  90.4 us
    gather x1, local copies, waits for them, and re-layouts, local(): jnp.take(vel_flat, got_cells, axis=1)  27.9 us
    gather x1, local copies, waits for them, and re-layouts, local(): near_high = jnp.take(vel_flat, cells + layer, axis=1)  27.9 us
    gather x1, local copies, waits for them, and re-layouts, local(): near_low = jnp.take(vel_flat, cells, axis=1)  27.8 us
    gather x1, local copies, waits for them, and re-layouts, local(): jnp.take(vel_flat, got_cells + layer, axis=1)  27.8 us
    ppermute x3, starting transfers between devices, shifted_2(): lax.ppermute(array, axis, [(i, (i + by) % peers) for i in range(peers)])  12.6 us
    unnamed x26, local copies, waits for them, and re-layouts  12.4 us
  transfers between devices with their start and end apart: 7, of which 3 were waited for; matrix products, arithmetic and copies ran while one was open for 42% of the time, Pallas kernels for 0%

commit v1 on v0

v1 whole, which is shorter than its diff:
```python
import jax
import jax.numpy as jnp
from jax import lax
from jax.experimental import pallas as pl
from jax.experimental.pallas import tpu as pltpu
from jax.sharding import PartitionSpec as P

VELOCITIES = [
    (0, 0, 0), (1, 0, 0), (-1, 0, 0), (0, 1, 0), (0, -1, 0), (0, 0, 1), (0, 0, -1),
    (1, 1, 0), (-1, -1, 0), (1, -1, 0), (-1, 1, 0), (1, 0, 1), (-1, 0, -1), (1, 0, -1),
    (-1, 0, 1), (0, 1, 1), (0, -1, -1), (0, 1, -1), (0, -1, 1),
]
WEIGHTS = [1.0 / 3.0] + [1.0 / 18.0] * 6 + [1.0 / 36.0] * 12
RATE2, RATE3, RATE4 = 1.6, 1.2, 1.4
STIFFNESS = 2.0

NZ, TX, TY = 8, 4, 128
BL, MK = 64, 128
CELLS = TX * NZ
F32, BF16 = jnp.float32, jnp.bfloat16
MESH = pl.DeviceIdType.MESH

XP = [i for i in range(19) if VELOCITIES[i][0] == 1]
XN = [i for i in range(19) if VELOCITIES[i][0] == -1]
YP = [i for i in range(19) if VELOCITIES[i][1] == 1]
YN = [i for i in range(19) if VELOCITIES[i][1] == -1]
HOPS = (-1, 0, 1, 2)
PEERS = [(t, s) for t in HOPS for s in (-1, 0, 1) if (t, s) != (0, 0)]


def opposite_of(i):
    return VELOCITIES.index(tuple(-c for c in VELOCITIES[i]))


def mirror_of(i):
    a, b, c = VELOCITIES[i]
    return VELOCITIES.index((a, b, -c))


def momentum_of(f):
    s = [f[2 * p + 1] + f[2 * p + 2] for p in range(9)]
    d = [f[2 * p + 1] - f[2 * p + 2] for p in range(9)]
    pxy, pxz, pyz = s[3] + s[4], s[5] + s[6], s[7] + s[8]
    density = f[0] + s[0] + s[1] + s[2] + pxy + pxz + pyz
    jx = d[0] + (d[3] + d[4]) + (d[5] + d[6])
    jy = d[1] + (d[3] - d[4]) + (d[7] + d[8])
    jz = d[2] + (d[5] - d[6]) + (d[7] - d[8])
    return s, d, density, jx, jy, jz


def collided(f):
    s, d, rho, jx, jy, jz = momentum_of(f)
    inv = 1.0 / rho
    ux, uy, uz = jx * inv, jy * inv, jz * inv
    ax, ay, az = jx * ux, jy * uy, jz * uz
    third, ninth = rho * (1.0 / 3.0), rho * (1.0 / 9.0)
    sixth = (ax + ay + az) * (1.0 / 6.0)
    pxy, pxz, pyz = s[3] + s[4], s[5] + s[6], s[7] + s[8]
    nxx = RATE2 * (s[0] + pxy + pxz - third - ax)
    nyy = RATE2 * (s[1] + pxy + pyz - third - ay)
    nzz = RATE2 * (s[2] + pxz + pyz - third - az)
    nxy = RATE2 * (s[3] - s[4] - jx * uy)
    nxz = RATE2 * (s[5] - s[6] - jx * uz)
    nyz = RATE2 * (s[7] - s[8] - jy * uz)
    tx, ty, tz = jx * (1.0 / 3.0), jy * (1.0 / 3.0), jz * (1.0 / 3.0)
    nxxy = RATE3 * (d[3] - d[4] - ty)
    nxyy = RATE3 * (d[3] + d[4] - tx)
    nxxz = RATE3 * (d[5] - d[6] - tz)
    nxzz = RATE3 * (d[5] + d[6] - tx)
    nyyz = RATE3 * (d[7] - d[8] - tz)
    nyzz = RATE3 * (d[7] + d[8] - ty)
    base = ninth - sixth
    qxy = RATE4 * (pxy - base - 0.5 * (ax + ay))
    qxz = RATE4 * (pxz - base - 0.5 * (ax + az))
    qyz = RATE4 * (pyz - base - 0.5 * (ay + az))
    even = [
        0.5 * (nxx - qxy - qxz), 0.5 * (nyy - qxy - qyz), 0.5 * (nzz - qxz - qyz),
        0.25 * (qxy + nxy), 0.25 * (qxy - nxy),
        0.25 * (qxz + nxz), 0.25 * (qxz - nxz),
        0.25 * (qyz + nyz), 0.25 * (qyz - nyz),
    ]
    odd = [
        -0.5 * (nxyy + nxzz), -0.5 * (nxxy + nyzz), -0.5 * (nxxz + nyyz),
        0.25 * (nxyy + nxxy), 0.25 * (nxyy - nxxy),
        0.25 * (nxzz + nxxz), 0.25 * (nxzz - nxxz),
        0.25 * (nyzz + nyyz), 0.25 * (nyzz - nyyz),
    ]
    out = [f[0] + (nxx + nyy + nzz - qxy - qxz - qyz)]
    for p in range(9):
        out.append(f[2 * p + 1] - (even[p] + odd[p]))
        out.append(f[2 * p + 2] - (even[p] - odd[p]))
    return out


def pushed(i, force):
    total = None
    for c, part in zip(VELOCITIES[i], force):
        if c != 0:
            term = part if c > 0 else -part
            total = term if total is None else total + term
    return None if total is None else (3.0 * WEIGHTS[i]) * total


def kernel(dist_h, cell_h, side_h, frac_h, blade_h, new_h, mf_h,
           dist_v, cell_v, side_v, frac_v, blade_v, new_v, mf_v,
           vel_n, vel_f, near_v, post_v, xs_p, xs_n, xr_m, xr_p,
           e_v, er_m1, er_m2, er_p1, ys_p, ys_n, yr_p, yr_n,
           in_sem, out_sem, v_sem, x_sem, e_sem, yp_sem, yn_sem):
    n_gx, n_gy = lax.axis_size("gx"), lax.axis_size("gy")
    gx, gy = lax.axis_index("gx"), lax.axis_index("gy")

    def peer(t, s):
        return (lax.rem(gx + t + n_gx, n_gx), lax.rem(gy + s + n_gy, n_gy))

    def remote(src, dst, sems, slot, t, s):
        return pltpu.make_async_remote_copy(
            src_ref=src, dst_ref=dst, send_sem=sems.at[0, slot], recv_sem=sems.at[1, slot],
            device_id=peer(t, s), device_id_type=MESH)

    loads = [pltpu.make_async_copy(h, v, in_sem.at[n]) for n, (h, v) in enumerate(
        ((dist_h, dist_v), (cell_h, cell_v), (side_h, side_v), (frac_h, frac_v), (blade_h, blade_v)))]
    for load in loads:
        load.start()
    barrier = pltpu.get_barrier_semaphore()
    for t, s in PEERS:
        pl.semaphore_signal(barrier, inc=1, device_id=peer(-t, -s), device_id_type=MESH)

    def rows(x):
        return pl.ds(x * NZ, NZ)

    def planes(x):
        return pl.ds(x, NZ, stride=TX)

    loads[0].wait()
    for x in range(TX):
        _, _, rho, jx, jy, jz = momentum_of([dist_v[i, planes(x), :] for i in range(19)])
        inv = 1.0 / rho
        for c, j in enumerate((jx, jy, jz)):
            vel_n[c, rows(x), :] = j * inv

    pl.semaphore_wait(barrier, len(PEERS))
    send_vel = remote(vel_n, vel_f, v_sem, 0, -1, 0)
    send_vel.start()

    for x in range(TX):
        post = collided([dist_v[i, planes(x), :] for i in range(19)])
        for i in range(19):
            post_v[i, rows(x), :] = post[i]
        if x == 0:
            for n, i in enumerate(XN):
                xs_n[n] = post[i]
        if x == TX - 1:
            for n, i in enumerate(XP):
                xs_p[n] = post[i]
    send_x = [remote(xs_p, xr_m, x_sem, 0, 1, 0), remote(xs_n, xr_p, x_sem, 1, -1, 0)]
    for copy in send_x:
        copy.start()

    lane = lax.broadcasted_iota(jnp.int32, (NZ, TY), 1)
    plane = lax.broadcasted_iota(jnp.int32, (NZ, TY), 0)

    def packed(blocks, column):
        total = None
        for n, block in enumerate(blocks):
            part = jnp.where(lane == plane + n * NZ, jnp.broadcast_to(block[:, column:column + 1], (NZ, TY)), 0.0)
            total = part if total is None else total + part
        return jnp.sum(total, axis=0, keepdims=True)

    for n, i in enumerate(YP):
        ys_p[3 + n:4 + n, :] = packed([post_v[i, rows(x), :] for x in range(TX)], TY - 1)
    for n, i in enumerate(YN):
        ys_n[3 + n:4 + n, :] = packed([post_v[i, rows(x), :] for x in range(TX)], 0)

    for load in loads[1:]:
        load.wait()

    def place(b):
        cell = cell_v[pl.ds(b * 8, 8), :]
        spot = cell & (TY - 1)
        row = ((cell >> 7) & (TX - 1)) * NZ + (cell >> 9)
        return spot, row

    def interpolated(table, b):
        spot, row = place(b)
        frac = frac_v[pl.ds(b * 8, 8), :]
        rest = 1.0 - frac
        total = [jnp.zeros((8, MK), F32) for _ in range(3)]
        for r in range(CELLS):
            weight = jnp.where(row == r, rest, jnp.where(row == r - 1, frac, 0.0))
            for c in range(3):
                line = jnp.broadcast_to(table[c, r:r + 1, :], (8, TY))
                total[c] = total[c] + weight * jnp.take_along_axis(line, spot, axis=1)
        return total

    def near_step(b, carry):
        found = interpolated(vel_n, b)
        for c in range(3):
            near_v[c, pl.ds(b * 8, 8), :] = found[c]
        return carry

    lax.fori_loop(0, BL // 8, near_step, 0, unroll=4)

    spots = lax.broadcasted_iota(jnp.int32, (TY, MK), 0).astype(F32).astype(BF16)
    lines = lax.broadcasted_iota(jnp.int32, (CELLS, MK), 0).astype(F32).astype(BF16)
    one, zero = jnp.ones((), BF16), jnp.zeros((), BF16)

    def spread(x, j, n):
        return jnp.broadcast_to(x[j:j + 1, :], (n, MK))

    def scatter(side, force_of):
        def step(b, total):
            spot, row = place(b)
            spot, row = spot.astype(F32).astype(BF16), row.astype(F32).astype(BF16)
            frac = frac_v[pl.ds(b * 8, 8), :]
            here = side_v[pl.ds(b * 8, 8), :] == side
            force = force_of(b)
            parts = []
            for c in range(3):
                own = jnp.where(here, force[c], 0.0)
                for value in ((1.0 - frac) * own, frac * own):
                    high = value.astype(BF16)
                    parts.append((high, (value - high.astype(F32)).astype(BF16)))
            hot = jnp.concatenate(
                [jnp.where(spots == spread(spot, j, TY), one, zero) for j in range(8)], axis=1)
            blocks = []
            for c in range(3):
                for h in range(2):
                    blocks.append(jnp.concatenate([
                        jnp.where(lines == spread(row, j, CELLS), spread(parts[2 * c][h], j, CELLS),
                                  jnp.where(lines == spread(row, j, CELLS) + 1,
                                            spread(parts[2 * c + 1][h], j, CELLS), zero))
                        for j in range(8)], axis=1))
            return total + lax.dot_general(jnp.concatenate(blocks, axis=0), hot, (((1,), (1,)), ((), ())),
                                           preferred_element_type=F32)
        total = lax.fori_loop(0, BL // 8, step, jnp.zeros((6 * CELLS, TY), F32), unroll=8)
        for c in range(3):
            e_v[c, side * CELLS:(side + 1) * CELLS, :] = (
                total[2 * c * CELLS:(2 * c + 1) * CELLS] + total[(2 * c + 1) * CELLS:(2 * c + 2) * CELLS])

    def near_force(b):
        return [STIFFNESS * (blade_v[c, pl.ds(b * 8, 8), :] - near_v[c, pl.ds(b * 8, 8), :]) for c in range(3)]

    scatter(0, near_force)

    send_vel.wait()

    def far_force(b):
        here = side_v[pl.ds(b * 8, 8), :] == 1
        found = interpolated(vel_f, b)
        force = []
        for c in range(3):
            vel = jnp.where(here, found[c], near_v[c, pl.ds(b * 8, 8), :])
            force.append(STIFFNESS * (blade_v[c, pl.ds(b * 8, 8), :] - vel))
            mf_v[c, pl.ds(b * 8, 8), :] = force[c]
        return force

    scatter(1, far_force)

    send_e = [remote(e_v.at[:, 3 * NZ:8 * NZ, :], er_m1, e_sem, 0, 1, 0),
              remote(e_v.at[:, 7 * NZ:8 * NZ, :], er_m2, e_sem, 1, 2, 0),
              remote(e_v.at[:, 0:NZ, :], er_p1, e_sem, 2, -1, 0)]
    for copy in send_e:
        copy.start()
    for c in range(3):
        blocks = [e_v[c, rows(x), :] for x in range(2 * TX)]
        ys_p[c:c + 1, :] = packed(blocks, TY - 1)
        ys_n[c:c + 1, :] = packed(blocks, 0)
    send_y = []
    for n, t in enumerate(HOPS):
        send_y.append(remote(ys_p, yr_p.at[n], yp_sem, n, t, 1))
        send_y.append(remote(ys_n, yr_n.at[n], yn_sem, n, t, -1))
    for copy in send_y:
        copy.start()
    store_mf = pltpu.make_async_copy(mf_v, mf_h, out_sem.at[0])
    store_mf.start()

    for copy in send_x + send_e + send_y:
        copy.wait()

    force = {}
    for x in range(-1, TX + 1):
        both = []
        for c in range(3):
            total = er_m1[c, pl.ds((x + 1) * NZ, NZ), :] if x < TX else er_p1[c]
            if x == -1:
                total = total + er_m2[c]
            else:
                total = total + e_v[c, rows(x), :]
            both.append(total)
        force[x] = both

    def edge(ref, group):
        total = None
        for n, t in enumerate(HOPS):
            part = pltpu.roll(ref[n], (NZ - NZ * TX * t) % TY, 1)
            total = part if total is None else total + part
        sides = [total[c:c + 1, :] for c in range(3)]
        return {i: total[3 + n:4 + n, :] + pushed(i, sides) for n, i in enumerate(group)}

    edges = edge(yr_p, YP)
    edges.update(edge(yr_n, YN))

    def post_at(i, x):
        if x == -1:
            value = xr_m[XP.index(i)]
        elif x == TX:
            value = xr_p[XN.index(i)]
        else:
            value = post_v[i, rows(x), :]
        push = pushed(i, force[x])
        return value if push is None else value + push

    def moved(i, x):
        value = post_at(i, x)
        cy = VELOCITIES[i][1]
        if cy == 0:
            return value
        column = jnp.sum(jnp.where(lane == plane + (x + 1) * NZ, jnp.broadcast_to(edges[i], (NZ, TY)), 0.0),
                         axis=1, keepdims=True)
        turned = pltpu.roll(value, cy % TY, 1)
        return jnp.where(lane == (0 if cy == 1 else TY - 1), jnp.broadcast_to(column, (NZ, TY)), turned)

    for x in range(TX):
        for i in range(19):
            cx, _, cz = VELOCITIES[i]
            value = moved(i, x - cx)
            if cz == 1:
                value = jnp.where(plane == 0, post_at(opposite_of(i), x), pltpu.roll(value, 1, 0))
            elif cz == -1:
                value = jnp.where(plane == NZ - 1, moved(mirror_of(i), x - cx), pltpu.roll(value, NZ - 1, 0))
            new_v[i, planes(x), :] = value

    store_new = pltpu.make_async_copy(new_v, new_h, out_sem.at[1])
    store_new.start()
    store_mf.wait()
    store_new.wait()


def local(dist, marker_cell, marker_side, marker_frac, blade_vel):
    hbm = pl.BlockSpec(memory_space=pl.ANY)
    field = pltpu.VMEM((3, CELLS, TY), F32)
    marks = pltpu.VMEM((3, BL, MK), F32)
    block = pltpu.VMEM((5, NZ, TY), F32)
    edge = pltpu.VMEM((8, TY), F32)
    dma = pltpu.SemaphoreType.DMA
    new, force = pl.pallas_call(
        kernel,
        out_shape=(jax.ShapeDtypeStruct((19, CELLS, TY), F32), jax.ShapeDtypeStruct((3, BL, MK), F32)),
        in_specs=[hbm] * 5,
        out_specs=(hbm, hbm),
        scratch_shapes=[
            pltpu.VMEM((19, CELLS, TY), F32), pltpu.VMEM((BL, MK), jnp.int32), pltpu.VMEM((BL, MK), jnp.int32),
            pltpu.VMEM((BL, MK), F32), marks, pltpu.VMEM((19, CELLS, TY), F32), marks,
            field, field, marks, pltpu.VMEM((19, CELLS, TY), F32), block, block, block, block,
            pltpu.VMEM((3, 2 * CELLS, TY), F32), pltpu.VMEM((3, 5 * NZ, TY), F32),
            pltpu.VMEM((3, NZ, TY), F32), pltpu.VMEM((3, NZ, TY), F32),
            edge, edge, pltpu.VMEM((4, 8, TY), F32), pltpu.VMEM((4, 8, TY), F32),
            dma((5,)), dma((2,)), dma((2, 1)), dma((2, 2)), dma((2, 3)), dma((2, 4)), dma((2, 4)),
        ],
        compiler_params=pltpu.CompilerParams(collective_id=0, has_side_effects=True),
        name="canopy_step",
    )(dist.reshape(19, CELLS, TY), marker_cell, marker_side, marker_frac, blade_vel)
    return new.reshape(dist.shape), force


def solution(mesh):
    return jax.shard_map(
        local,
        mesh=mesh,
        in_specs=(
            P(None, None, "gx", "gy"),
            P(("gx", "gy"), None),
            P(("gx", "gy"), None),
            P(("gx", "gy"), None),
            P(None, ("gx", "gy"), None),
        ),
        out_specs=(P(None, None, "gx", "gy"), P(None, ("gx", "gy"), None)),
        check_vma=False,
    )
```

time: 415 us -> 29.9 us (0.07); the launches traced: 409 us -> 29.7 us
  other arithmetic: 224 us -> 0 us
  local copies, waits for them, and re-layouts: 144 us -> 2.39 us
  starting transfers between devices: 32 us -> 0 us
  Pallas kernels: 0 us -> 26.7 us
  matrix products: 5.6 us -> 0 us
    scatter-add x4 -> x0, other arithmetic: 192 us -> none  [the longest x2 102 us: local(): force = empty.at[:, cells].add(own_low).at[:, cells + layer].add(own_high)]
    gather x4 -> x0, local copies, waits for them, and re-layouts: 111 us -> none  [the longest x1 27.9 us: local(): jnp.take(vel_flat, got_cells, axis=1)]
    ppermute x7 -> x0, starting transfers between devices: 32 us -> none  [the longest x3 12.6 us: shifted_2(): lax.ppermute(array, axis, [(i, (i + by) % peers) for i in range(peers)])]
    pallas_call x0 -> x1, Pallas kernels: none -> 26.7 us  [local(): pl.pallas_call(kernel, out_shape=(jax.ShapeDtypeStruct((19, CELLS, TY), F...]
    another operation x6 -> x0, other arithmetic: 15.6 us -> none  [the longest x2 7.82 us: local(): jnp.stack([jnp.take(vel_flat, got_cells, axis=1), jnp.take(vel_flat, got_...]
    mul x3 -> x0, other arithmetic: 12.1 us -> none  [the longest x1 11.3 us: local(): pushes = STIFFNESS * (pushes_goal - marker_velocity)]
    another operation x4 -> x0, local copies, waits for them, and re-layouts: 11.4 us -> none  [the longest x2 5.71 us: local(): jnp.stack([jnp.take(vel_flat, got_cells, axis=1), jnp.take(vel_flat, got_...]
    unnamed x26 -> x4, local copies, waits for them, and re-layouts: 12.4 us -> 2.39 us
  transfers between devices with their start and end apart: 7 -> 0, of which waited for: 3 -> 0; matrix products, arithmetic and copies ran while one was open for 42% -> 0% of each run, Pallas kernels for 0% -> 0%
where the time goes in v1:
time: 29.9 us; the launch traced here: 29.7 us
  Pallas kernels  26.7 us (89%)
  local copies, waits for them, and re-layouts  2.39 us (8%)
  between operations  0.65 us (2%)
    pallas_call x1, Pallas kernels, local(): pl.pallas_call(kernel, out_shape=(jax.ShapeDtypeStruct((19, CELLS, TY), F...  26.7 us
    unnamed x4, local copies, waits for them, and re-layouts  2.39 us

profile of v1, /device:TPU:1, one launch (start us, length us, event | category | flops | bytes accessed | tf_op | source)
XLA Modules:
  0.0 29.7 jit_solution(17222045642808065085)
XLA Ops:
  0.6 26.7 %canopy_step.1 = (f32[19,32,128]{2,1,0:T(8,128)}, f32[3,64,128]{2,1,0:T(8,128)}) custom-call(f32[19,32,128]{2,1,0:T(8,128)} %bitcast.3, s32[64,128]{1,0:T(8,128)} %cell_h.1, s32[64,128]{1,0:T(8,128)} %side_h.1, f32[64,128]{1,0:T(8,128)} %frac_h.1, f32[3,64,128]{2,1,0:T(8,128)} %blade_h.1), custom_call_target="tpu_custom_call" | custom-call | tf_op jit(solution)/shard_map/canopy_step/pallas_call | solution.py:346
  27.3 0.0 copy-start
  27.3 1.7 %copy.9 = f32[19,8,4,128]{3,2,1,0:T(4,128)} copy(f32[19,8,4,128]{3,2,1,0:T(4,128)} %bitcast.2) | data formatting | bytes 622592
  29.1 0.0 copy-done
  29.1 0.6 %copy.10 = f32[3,64,128]{2,1,0:T(8,128)} copy(f32[3,64,128]{2,1,0:T(8,128)S(1)} %copy-done) | data formatting | bytes 196608
Async XLA Ops:
  27.3 1.8 %copy-start = (f32[3,64,128]{2,1,0:T(8,128)S(1)}, f32[3,64,128]{2,1,0:T(8,128)}, u32[]{:S(2)}) copy-start(f32[3,64,128]{2,1,0:T(8,128)} %get-tuple-element.9) | copy-start | bytes 294916

commit v2 on v1

--- a/solution.py
+++ b/solution.py
@@ -101,11 +101,33 @@
     return None if total is None else (3.0 * WEIGHTS[i]) * total
 
 
-def kernel(dist_h, cell_h, side_h, frac_h, blade_h, new_h, mf_h,
-           dist_v, cell_v, side_v, frac_v, blade_v, new_v, mf_v,
-           vel_n, vel_f, near_v, post_v, xs_p, xs_n, xr_m, xr_p,
-           e_v, er_m1, er_m2, er_p1, ys_p, ys_n, yr_p, yr_n,
-           in_sem, out_sem, v_sem, x_sem, e_sem, yp_sem, yn_sem):
+def rows(x):
+    return pl.ds(x * NZ, NZ)
+
+
+def planes(x):
+    return pl.ds(x, NZ, stride=TX)
+
+
+def lanes_and_planes():
+    return (lax.broadcasted_iota(jnp.int32, (NZ, TY), 1), lax.broadcasted_iota(jnp.int32, (NZ, TY), 0))
+
+
+def packed(blocks, column, first=0):
+    lane, plane = lanes_and_planes()
+    total = None
+    for n, block in enumerate(blocks):
+        part = jnp.where(lane == plane + (first + n) * NZ,
+                         jnp.broadcast_to(block[:, column:column + 1], (NZ, TY)), 0.0)
+        total = part if total is None else total + part
+    return jnp.sum(total, axis=0, keepdims=True)
+
+
+def exchange(dist_h, cell_h, side_h, frac_h, blade_h, new_v, mf_v, yr_p, yr_n,
+             dist_v, cell_v, side_v, frac_v, blade_v,
+             vel_n, vel_f, near_v, post_v, xs_p, xs_n, xr_m, xr_p,
+             e_v, er_m1, er_m2, ys_p, ys_n,
+             in_sem, v_sem, x_sem, e_sem, yp_sem, yn_sem):
     n_gx, n_gy = lax.axis_size("gx"), lax.axis_size("gy")
     gx, gy = lax.axis_index("gx"), lax.axis_index("gy")
 
@@ -117,19 +139,13 @@
             src_ref=src, dst_ref=dst, send_sem=sems.at[0, slot], recv_sem=sems.at[1, slot],
             device_id=peer(t, s), device_id_type=MESH)
 
+    barrier = pltpu.get_barrier_semaphore()
+    for t, s in PEERS:
+        pl.semaphore_signal(barrier, inc=1, device_id=peer(-t, -s), device_id_type=MESH)
     loads = [pltpu.make_async_copy(h, v, in_sem.at[n]) for n, (h, v) in enumerate(
         ((dist_h, dist_v), (cell_h, cell_v), (side_h, side_v), (frac_h, frac_v), (blade_h, blade_v)))]
     for load in loads:
         load.start()
-    barrier = pltpu.get_barrier_semaphore()
-    for t, s in PEERS:
-        pl.semaphore_signal(barrier, inc=1, device_id=peer(-t, -s), device_id_type=MESH)
-
-    def rows(x):
-        return pl.ds(x * NZ, NZ)
-
-    def planes(x):
-        return pl.ds(x, NZ, stride=TX)
 
     loads[0].wait()
     for x in range(TX):
@@ -152,20 +168,6 @@
         if x == TX - 1:
             for n, i in enumerate(XP):
                 xs_p[n] = post[i]
-    send_x = [remote(xs_p, xr_m, x_sem, 0, 1, 0), remote(xs_n, xr_p, x_sem, 1, -1, 0)]
-    for copy in send_x:
-        copy.start()
-
-    lane = lax.broadcasted_iota(jnp.int32, (NZ, TY), 1)
-    plane = lax.broadcasted_iota(jnp.int32, (NZ, TY), 0)
-
-    def packed(blocks, column):
-        total = None
-        for n, block in enumerate(blocks):
-            part = jnp.where(lane == plane + n * NZ, jnp.broadcast_to(block[:, column:column + 1], (NZ, TY)), 0.0)
-            total = part if total is None else total + part
-        return jnp.sum(total, axis=0, keepdims=True)
-
     for n, i in enumerate(YP):
         ys_p[3 + n:4 + n, :] = packed([post_v[i, rows(x), :] for x in range(TX)], TY - 1)
     for n, i in enumerate(YN):
@@ -191,14 +193,6 @@
                 line = jnp.broadcast_to(table[c, r:r + 1, :], (8, TY))
                 total[c] = total[c] + weight * jnp.take_along_axis(line, spot, axis=1)
         return total
-
-    def near_step(b, carry):
-        found = interpolated(vel_n, b)
-        for c in range(3):
-            near_v[c, pl.ds(b * 8, 8), :] = found[c]
-        return carry
-
-    lax.fori_loop(0, BL // 8, near_step, 0, unroll=4)
 
     spots = lax.broadcasted_iota(jnp.int32, (TY, MK), 0).astype(F32).astype(BF16)
     lines = lax.broadcasted_iota(jnp.int32, (CELLS, MK), 0).astype(F32).astype(BF16)
@@ -238,9 +232,21 @@
                 total[2 * c * CELLS:(2 * c + 1) * CELLS] + total[(2 * c + 1) * CELLS:(2 * c + 2) * CELLS])
 
     def near_force(b):
-        return [STIFFNESS * (blade_v[c, pl.ds(b * 8, 8), :] - near_v[c, pl.ds(b * 8, 8), :]) for c in range(3)]
+        found = interpolated(vel_n, b)
+        for c in range(3):
+            near_v[c, pl.ds(b * 8, 8), :] = found[c]
+        return [STIFFNESS * (blade_v[c, pl.ds(b * 8, 8), :] - found[c]) for c in range(3)]
 
     scatter(0, near_force)
+    for c in range(3):
+        blocks = [e_v[c, rows(x), :] for x in range(TX)]
+        xs_n[5 + c] = blocks[0]
+        xs_p[5 + c] = blocks[-1]
+        ys_p[c:c + 1, :] = packed(blocks, TY - 1)
+        ys_n[c:c + 1, :] = packed(blocks, 0)
+    send_x = [remote(xs_p, xr_m, x_sem, 0, 1, 0), remote(xs_n, xr_p, x_sem, 1, -1, 0)]
+    for copy in send_x:
+        copy.start()
 
     send_vel.wait()
 
@@ -256,49 +262,30 @@
 
     scatter(1, far_force)
 
-    send_e = [remote(e_v.at[:, 3 * NZ:8 * NZ, :], er_m1, e_sem, 0, 1, 0),
-              remote(e_v.at[:, 7 * NZ:8 * NZ, :], er_m2, e_sem, 1, 2, 0),
-              remote(e_v.at[:, 0:NZ, :], er_p1, e_sem, 2, -1, 0)]
-    for copy in send_e:
-        copy.start()
     for c in range(3):
-        blocks = [e_v[c, rows(x), :] for x in range(2 * TX)]
-        ys_p[c:c + 1, :] = packed(blocks, TY - 1)
-        ys_n[c:c + 1, :] = packed(blocks, 0)
+        blocks = [e_v[c, rows(x), :] for x in range(TX, 2 * TX)]
+        ys_p[c:c + 1, :] = ys_p[c:c + 1, :] + packed(blocks, TY - 1, TX)
+        ys_n[c:c + 1, :] = ys_n[c:c + 1, :] + packed(blocks, 0, TX)
     send_y = []
-    for n, t in enumerate(HOPS):
+    for n, t in reversed(list(enumerate(HOPS))):
         send_y.append(remote(ys_p, yr_p.at[n], yp_sem, n, t, 1))
         send_y.append(remote(ys_n, yr_n.at[n], yn_sem, n, t, -1))
     for copy in send_y:
         copy.start()
-    store_mf = pltpu.make_async_copy(mf_v, mf_h, out_sem.at[0])
-    store_mf.start()
-
-    for copy in send_x + send_e + send_y:
+    send_e = [remote(e_v.at[:, CELLS:, :], er_m1, e_sem, 0, 1, 0),
+              remote(e_v.at[:, 2 * CELLS - NZ:, :], er_m2, e_sem, 1, 2, 0)]
+    for copy in send_e:
+        copy.start()
+
+    for copy in send_x + send_e:
         copy.wait()
 
-    force = {}
-    for x in range(-1, TX + 1):
-        both = []
-        for c in range(3):
-            total = er_m1[c, pl.ds((x + 1) * NZ, NZ), :] if x < TX else er_p1[c]
-            if x == -1:
-                total = total + er_m2[c]
-            else:
-                total = total + e_v[c, rows(x), :]
-            both.append(total)
-        force[x] = both
-
-    def edge(ref, group):
-        total = None
-        for n, t in enumerate(HOPS):
-            part = pltpu.roll(ref[n], (NZ - NZ * TX * t) % TY, 1)
-            total = part if total is None else total + part
-        sides = [total[c:c + 1, :] for c in range(3)]
-        return {i: total[3 + n:4 + n, :] + pushed(i, sides) for n, i in enumerate(group)}
-
-    edges = edge(yr_p, YP)
-    edges.update(edge(yr_n, YN))
+    force = {-1: [er_m2[c] + xr_m[5 + c] for c in range(3)],
+             TX: [e_v[c, rows(TX), :] + xr_p[5 + c] for c in range(3)]}
+    for x in range(TX):
+        force[x] = [e_v[c, rows(x), :] + er_m1[c, rows(x), :] for c in range(3)]
+
+    _, plane = lanes_and_planes()
 
     def post_at(i, x):
         if x == -1:
@@ -313,12 +300,7 @@
     def moved(i, x):
         value = post_at(i, x)
         cy = VELOCITIES[i][1]
-        if cy == 0:
-            return value
-        column = jnp.sum(jnp.where(lane == plane + (x + 1) * NZ, jnp.broadcast_to(edges[i], (NZ, TY)), 0.0),
-                         axis=1, keepdims=True)
-        turned = pltpu.roll(value, cy % TY, 1)
-        return jnp.where(lane == (0 if cy == 1 else TY - 1), jnp.broadcast_to(column, (NZ, TY)), turned)
+        return value if cy == 0 else pltpu.roll(value, cy % TY, 1)
 
     for x in range(TX):
         for i in range(19):
@@ -330,36 +312,88 @@
                 value = jnp.where(plane == NZ - 1, moved(mirror_of(i), x - cx), pltpu.roll(value, NZ - 1, 0))
             new_v[i, planes(x), :] = value
 
-    store_new = pltpu.make_async_copy(new_v, new_h, out_sem.at[1])
-    store_new.start()
-    store_mf.wait()
-    store_new.wait()
+    for copy in send_y:
+        copy.wait()
+
+
+def finish(mid, mf, yr_p, yr_n, new_h, mf_h, new_v, sem):
+    straight = [i for i in range(19) if VELOCITIES[i][1] == 0]
+    copies = [pltpu.make_async_copy(mid.at[i], new_h.at[i], sem.at[i]) for i in straight]
+    copies.append(pltpu.make_async_copy(mf, mf_h, sem.at[19]))
+    for copy in copies:
+        copy.start()
+    lane, plane = lanes_and_planes()
+
+    def edge(ref, group):
+        total = None
+        for n, t in enumerate(HOPS):
+            part = pltpu.roll(ref[n], (NZ - NZ * TX * t) % TY, 1)
+            total = part if total is None else total + part
+        sides = [total[c:c + 1, :] for c in range(3)]
+        return {i: total[3 + n:4 + n, :] + pushed(i, sides) for n, i in enumerate(group)}
+
+    edges = edge(yr_p, YP)
+    edges.update(edge(yr_n, YN))
+
+    def column(i, x):
+        spot = lane == plane + (x + 1) * NZ
+        return jnp.broadcast_to(
+            jnp.sum(jnp.where(spot, jnp.broadcast_to(edges[i], (NZ, TY)), 0.0), axis=1, keepdims=True), (NZ, TY))
+
+    for i in YP + YN:
+        cx, cy, cz = VELOCITIES[i]
+        last = 0 if cy == 1 else TY - 1
+        for x in range(TX):
+            value = column(i, x - cx)
+            if cz == 1:
+                value = pltpu.roll(value, 1, 0)
+                here = jnp.logical_and(lane == last, plane > 0)
+            elif cz == -1:
+                value = jnp.where(plane == NZ - 1, column(mirror_of(i), x - cx), pltpu.roll(value, NZ - 1, 0))
+                here = lane == last
+            else:
+                here = lane == last
+            new_v[i, planes(x), :] = jnp.where(here, value, mid[i, planes(x), :])
+        copy = pltpu.make_async_copy(new_v.at[i], new_h.at[i], sem.at[i])
+        copy.start()
+        copies.append(copy)
+    for copy in copies:
+        copy.wait()
 
 
 def local(dist, marker_cell, marker_side, marker_frac, blade_vel):
-    hbm = pl.BlockSpec(memory_space=pl.ANY)
+    hbm = pl.BlockSpec(memory_space=pltpu.HBM)
+    vmem = pl.BlockSpec(memory_space=pltpu.VMEM)
+    cells = pltpu.VMEM((19, CELLS, TY), F32)
     field = pltpu.VMEM((3, CELLS, TY), F32)
     marks = pltpu.VMEM((3, BL, MK), F32)
-    block = pltpu.VMEM((5, NZ, TY), F32)
+    block = pltpu.VMEM((8, NZ, TY), F32)
     edge = pltpu.VMEM((8, TY), F32)
     dma = pltpu.SemaphoreType.DMA
+    shape = jax.ShapeDtypeStruct
+    mid, mf, yr_p, yr_n = pl.pallas_call(
+        exchange,
+        out_shape=(shape((19, CELLS, TY), F32), shape((3, BL, MK), F32), shape((4, 8, TY), F32), shape((4, 8, TY), F32)),
+        in_specs=[hbm] * 5,
+        out_specs=(vmem,) * 4,
+        scratch_shapes=[
+            cells, pltpu.VMEM((BL, MK), jnp.int32), pltpu.VMEM((BL, MK), jnp.int32), pltpu.VMEM((BL, MK), F32), marks,
+            field, field, marks, cells, block, block, block, block,
+            pltpu.VMEM((3, 2 * CELLS, TY), F32), field, pltpu.VMEM((3, NZ, TY), F32), edge, edge,
+            dma((5,)), dma((2, 1)), dma((2, 2)), dma((2, 2)), dma((2, 4)), dma((2, 4)),
+        ],
+        compiler_params=pltpu.CompilerParams(collective_id=0, has_side_effects=True, vmem_limit_bytes=32 * 2**20),
+        name="exchange",
+    )(*(pltpu.with_memory_space_constraint(a, pltpu.HBM) for a in (dist.reshape(19, CELLS, TY), marker_cell, marker_side, marker_frac, blade_vel)))
     new, force = pl.pallas_call(
-        kernel,
-        out_shape=(jax.ShapeDtypeStruct((19, CELLS, TY), F32), jax.ShapeDtypeStruct((3, BL, MK), F32)),
-        in_specs=[hbm] * 5,
+        finish,
+        out_shape=(shape((19, CELLS, TY), F32), shape((3, BL, MK), F32)),
+        in_specs=[vmem] * 4,
         out_specs=(hbm, hbm),
-        scratch_shapes=[
-            pltpu.VMEM((19, CELLS, TY), F32), pltpu.VMEM((BL, MK), jnp.int32), pltpu.VMEM((BL, MK), jnp.int32),
-            pltpu.VMEM((BL, MK), F32), marks, pltpu.VMEM((19, CELLS, TY), F32), marks,
-            field, field, marks, pltpu.VMEM((19, CELLS, TY), F32), block, block, block, block,
-            pltpu.VMEM((3, 2 * CELLS, TY), F32), pltpu.VMEM((3, 5 * NZ, TY), F32),
-            pltpu.VMEM((3, NZ, TY), F32), pltpu.VMEM((3, NZ, TY), F32),
-            edge, edge, pltpu.VMEM((4, 8, TY), F32), pltpu.VMEM((4, 8, TY), F32),
-            dma((5,)), dma((2,)), dma((2, 1)), dma((2, 2)), dma((2, 3)), dma((2, 4)), dma((2, 4)),
-        ],
-        compiler_params=pltpu.CompilerParams(collective_id=0, has_side_effects=True),
-        name="canopy_step",
-    )(dist.reshape(19, CELLS, TY), marker_cell, marker_side, marker_frac, blade_vel)
+        scratch_shapes=[cells, dma((20,))],
+        compiler_params=pltpu.CompilerParams(vmem_limit_bytes=16 * 2**20),
+        name="finish",
+    )(mid, mf, yr_p, yr_n)
     return new.reshape(dist.shape), force
 
 

time: 29.9 us -> 27.2 us (0.910)
  local copies, waits for them, and re-layouts: 2.39 us -> 0 us
  Pallas kernels: 26.7 us -> 26.4 us
    unnamed x4 -> x0, local copies, waits for them, and re-layouts: 2.39 us -> none
    pallas_call x1 -> x2, Pallas kernels: 26.7 us -> 26.4 us  [the longest x1 25.4 us: local(): pl.pallas_call(exchange, out_shape=(shape((19, CELLS, TY), F32), shape((3...]
where the time goes in v2:
time: 27.2 us; the launch traced here: 27.1 us
  Pallas kernels  26.4 us (97%)
  between operations  0.64 us (2%)
    pallas_call x1, Pallas kernels, local(): pl.pallas_call(exchange, out_shape=(shape((19, CELLS, TY), F32), shape((3...  25.4 us
    pallas_call x1, Pallas kernels, local(): pl.pallas_call(finish, out_shape=(shape((19, CELLS, TY), F32), shape((3,...  1 us

profile of v2, /device:TPU:1, one launch (start us, length us, event | category | flops | bytes accessed | tf_op | source)
XLA Modules:
  0.0 27.1 jit_solution(16903734907979161184)
XLA Ops:
  0.6 25.4 %exchange.1 = (f32[19,32,128]{2,1,0:T(8,128)S(1)}, f32[3,64,128]{2,1,0:T(8,128)S(1)}, f32[4,8,128]{2,1,0:T(8,128)S(1)}, f32[4,8,128]{2,1,0:T(8,128)S(1)}) custom-call(f32[19,32,128]{2,1,0:T(8,128)} %bitcast.2, s32[64,128]{1,0:T(8,128)} %cell_h.1, s32[64,128]{1,0:T(8,128)} %side_h.1, f32[64,128]{1,0:T(8,128)} %frac_h.1, f32[3,64,128]{2,1,0:T(8,128)} %blade_h.1), custom_call_target="tpu_custom_call" | custom-call | tf_op jit(solution)/shard_map/exchange/pallas_call | solution.py:374
  26.1 1.0 %finish.1 = (f32[19,32,128]{2,1,0:T(8,128)}, f32[3,64,128]{2,1,0:T(8,128)}) custom-call(f32[19,32,128]{2,1,0:T(8,128)S(1)} %get-tuple-element.8.mid, f32[3,64,128]{2,1,0:T(8,128)S(1)} %get-tuple-element.9.mf, f32[4,8,128]{2,1,0:T(8,128)S(1)} %get-tuple-element.10.yr_p, f32[4,8,128]{2,1,0:T(8,128)S(1)} %get-tuple-element.11.yr_n), custom_call_target="tpu_custom_call" | custom-call | tf_op jit(solution)/shard_map/finish/pallas_call | solution.py:388

commit v3 on v2

v3 whole, which is shorter than its diff:
```python
import jax
import jax.numpy as jnp
from jax import lax
from jax.experimental import pallas as pl
from jax.experimental.pallas import tpu as pltpu
from jax.sharding import PartitionSpec as P

VELOCITIES = [
    (0, 0, 0), (1, 0, 0), (-1, 0, 0), (0, 1, 0), (0, -1, 0), (0, 0, 1), (0, 0, -1),
    (1, 1, 0), (-1, -1, 0), (1, -1, 0), (-1, 1, 0), (1, 0, 1), (-1, 0, -1), (1, 0, -1),
    (-1, 0, 1), (0, 1, 1), (0, -1, -1), (0, 1, -1), (0, -1, 1),
]
WEIGHTS = [1.0 / 3.0] + [1.0 / 18.0] * 6 + [1.0 / 36.0] * 12
RATE2, RATE3, RATE4 = 1.6, 1.2, 1.4
STIFFNESS = 2.0

NZ, TX, TY = 8, 4, 128
BL, MK = 64, 128
CELLS = TX * NZ
F32, BF16 = jnp.float32, jnp.bfloat16
MESH = pl.DeviceIdType.MESH

XP = [i for i in range(19) if VELOCITIES[i][0] == 1]
XN = [i for i in range(19) if VELOCITIES[i][0] == -1]
YP = [i for i in range(19) if VELOCITIES[i][1] == 1]
YN = [i for i in range(19) if VELOCITIES[i][1] == -1]
HOPS = (-1, 0, 1, 2)
PEERS = [(t, s) for t in HOPS for s in (-1, 0, 1) if (t, s) != (0, 0)]


def opposite_of(i):
    return VELOCITIES.index(tuple(-c for c in VELOCITIES[i]))


def mirror_of(i):
    a, b, c = VELOCITIES[i]
    return VELOCITIES.index((a, b, -c))


def momentum_of(f):
    s = [f[2 * p + 1] + f[2 * p + 2] for p in range(9)]
    d = [f[2 * p + 1] - f[2 * p + 2] for p in range(9)]
    pxy, pxz, pyz = s[3] + s[4], s[5] + s[6], s[7] + s[8]
    density = f[0] + s[0] + s[1] + s[2] + pxy + pxz + pyz
    jx = d[0] + (d[3] + d[4]) + (d[5] + d[6])
    jy = d[1] + (d[3] - d[4]) + (d[7] + d[8])
    jz = d[2] + (d[5] - d[6]) + (d[7] - d[8])
    return s, d, density, jx, jy, jz


def collided(f):
    s, d, rho, jx, jy, jz = momentum_of(f)
    inv = 1.0 / rho
    ux, uy, uz = jx * inv, jy * inv, jz * inv
    ax, ay, az = jx * ux, jy * uy, jz * uz
    third, ninth = rho * (1.0 / 3.0), rho * (1.0 / 9.0)
    sixth = (ax + ay + az) * (1.0 / 6.0)
    pxy, pxz, pyz = s[3] + s[4], s[5] + s[6], s[7] + s[8]
    nxx = RATE2 * (s[0] + pxy + pxz - third - ax)
    nyy = RATE2 * (s[1] + pxy + pyz - third - ay)
    nzz = RATE2 * (s[2] + pxz + pyz - third - az)
    nxy = RATE2 * (s[3] - s[4] - jx * uy)
    nxz = RATE2 * (s[5] - s[6] - jx * uz)
    nyz = RATE2 * (s[7] - s[8] - jy * uz)
    tx, ty, tz = jx * (1.0 / 3.0), jy * (1.0 / 3.0), jz * (1.0 / 3.0)
    nxxy = RATE3 * (d[3] - d[4] - ty)
    nxyy = RATE3 * (d[3] + d[4] - tx)
    nxxz = RATE3 * (d[5] - d[6] - tz)
    nxzz = RATE3 * (d[5] + d[6] - tx)
    nyyz = RATE3 * (d[7] - d[8] - tz)
    nyzz = RATE3 * (d[7] + d[8] - ty)
    base = ninth - sixth
    qxy = RATE4 * (pxy - base - 0.5 * (ax + ay))
    qxz = RATE4 * (pxz - base - 0.5 * (ax + az))
    qyz = RATE4 * (pyz - base - 0.5 * (ay + az))
    even = [
        0.5 * (nxx - qxy - qxz), 0.5 * (nyy - qxy - qyz), 0.5 * (nzz - qxz - qyz),
        0.25 * (qxy + nxy), 0.25 * (qxy - nxy),
        0.25 * (qxz + nxz), 0.25 * (qxz - nxz),
        0.25 * (qyz + nyz), 0.25 * (qyz - nyz),
    ]
    odd = [
        -0.5 * (nxyy + nxzz), -0.5 * (nxxy + nyzz), -0.5 * (nxxz + nyyz),
        0.25 * (nxyy + nxxy), 0.25 * (nxyy - nxxy),
        0.25 * (nxzz + nxxz), 0.25 * (nxzz - nxxz),
        0.25 * (nyzz + nyyz), 0.25 * (nyzz - nyyz),
    ]
    out = [f[0] + (nxx + nyy + nzz - qxy - qxz - qyz)]
    for p in range(9):
        out.append(f[2 * p + 1] - (even[p] + odd[p]))
        out.append(f[2 * p + 2] - (even[p] - odd[p]))
    return out


def pushed(i, force):
    total = None
    for c, part in zip(VELOCITIES[i], force):
        if c != 0:
            term = part if c > 0 else -part
            total = term if total is None else total + term
    return None if total is None else (3.0 * WEIGHTS[i]) * total


def rows(x):
    return pl.ds(x * NZ, NZ)


def planes(x):
    return pl.ds(x, NZ, stride=TX)


def lanes_and_planes():
    return (lax.broadcasted_iota(jnp.int32, (NZ, TY), 1), lax.broadcasted_iota(jnp.int32, (NZ, TY), 0))


def packed(blocks, column):
    lane, plane = lanes_and_planes()
    total = None
    for n, block in enumerate(blocks):
        part = jnp.where(lane == plane + n * NZ, jnp.broadcast_to(block[:, column:column + 1], (NZ, TY)), 0.0)
        total = part if total is None else total + part
    return jnp.sum(total, axis=0, keepdims=True)


def force_of(fields, vel, axis):
    size = vel[0].shape[axis]
    out = []
    for c in range(3):
        below = pltpu.roll(fields[4] * vel[c], 1, axis)
        above = fields[4] * pltpu.roll(vel[c], size - 1, axis)
        out.append(STIFFNESS * (fields[c] - fields[3] * vel[c] - above - below))
    return out


def exchange(dist_h, cell_h, side_h, frac_h, blade_h, new_v, mf_v, yr_p, yr_n,
             dist_v, cell_v, side_v, frac_v, blade_v,
             vel_n, vel_f, post_v, xs_p, xs_n, xr_m, xr_p,
             g_v, gr_1, gr_2, ys_p, ys_n,
             in_sem, v_sem, x_sem, g_sem, yp_sem, yn_sem):
    n_gx, n_gy = lax.axis_size("gx"), lax.axis_size("gy")
    gx, gy = lax.axis_index("gx"), lax.axis_index("gy")

    def peer(t, s):
        return (lax.rem(gx + t + n_gx, n_gx), lax.rem(gy + s + n_gy, n_gy))

    def remote(src, dst, sems, slot, t, s):
        return pltpu.make_async_remote_copy(
            src_ref=src, dst_ref=dst, send_sem=sems.at[0, slot], recv_sem=sems.at[1, slot],
            device_id=peer(t, s), device_id_type=MESH)

    barrier = pltpu.get_barrier_semaphore()
    for t, s in PEERS:
        pl.semaphore_signal(barrier, inc=1, device_id=peer(-t, -s), device_id_type=MESH)
    loads = [pltpu.make_async_copy(h, v, in_sem.at[n]) for n, (h, v) in enumerate(
        ((cell_h, cell_v), (side_h, side_v), (frac_h, frac_v), (blade_h, blade_v), (dist_h, dist_v)))]
    for load in loads:
        load.start()
    for load in loads:
        load.wait()

    for x in range(TX):
        values = [dist_v[i, planes(x), :] for i in range(19)]
        _, _, rho, jx, jy, jz = momentum_of(values)
        inv = 1.0 / rho
        for c, j in enumerate((jx, jy, jz)):
            vel_n[c, rows(x), :] = j * inv
        for i, post in enumerate(collided(values)):
            post_v[i, rows(x), :] = post

    spots = lax.broadcasted_iota(jnp.int32, (2 * TY, MK), 0).astype(F32).astype(BF16)
    lines = lax.broadcasted_iota(jnp.int32, (CELLS, MK), 0).astype(F32).astype(BF16)
    one, zero = jnp.ones((), BF16), jnp.zeros((), BF16)

    def spread(x, j, n):
        return jnp.broadcast_to(x[j:j + 1, :], (n, MK))

    def place(b):
        cell = cell_v[pl.ds(b * 8, 8), :]
        spot = cell & (TY - 1)
        row = ((cell >> 7) & (TX - 1)) * NZ + (cell >> 9)
        return spot, row

    def halves(value):
        high = value.astype(BF16)
        return high, (value - high.astype(F32)).astype(BF16)

    def scatter_step(b, total):
        spot, row = place(b)
        spot = (spot + side_v[pl.ds(b * 8, 8), :] * TY).astype(F32).astype(BF16)
        row = row.astype(F32).astype(BF16)
        frac = frac_v[pl.ds(b * 8, 8), :]
        rest = 1.0 - frac
        pairs = []
        for c in range(3):
            blade = blade_v[c, pl.ds(b * 8, 8), :]
            pairs.append((halves(rest * blade), halves(frac * blade)))
        pairs.append((halves(rest * rest), halves(frac * frac)))
        pairs.append((halves(rest * frac), None))
        hot = jnp.concatenate([jnp.where(spots == spread(spot, j, 2 * TY), one, zero) for j in range(8)], axis=1)
        blocks = []
        for low, high in pairs:
            for h in range(2):
                parts = []
                for j in range(8):
                    line = spread(row, j, CELLS)
                    upper = zero if high is None else jnp.where(lines == line + 1, spread(high[h], j, CELLS), zero)
                    parts.append(jnp.where(lines == line, spread(low[h], j, CELLS), upper))
                blocks.append(jnp.concatenate(parts, axis=1))
        return total + lax.dot_general(jnp.concatenate(blocks, axis=0), hot, (((1,), (1,)), ((), ())),
                                       preferred_element_type=F32)

    total = lax.fori_loop(0, BL // 8, scatter_step, jnp.zeros((10 * CELLS, 2 * TY), F32), unroll=8)
    for n in range(5):
        both = total[2 * n * CELLS:(2 * n + 1) * CELLS] + total[(2 * n + 1) * CELLS:(2 * n + 2) * CELLS]
        g_v[n, 0:CELLS, :] = both[:, :TY]
        g_v[n, CELLS:2 * CELLS, :] = both[:, TY:]

    ys_p[...] = jnp.zeros_like(ys_p)
    ys_n[...] = jnp.zeros_like(ys_n)
    for n in range(5):
        blocks = [g_v[n, rows(x), :] for x in range(2 * TX)]
        ys_p[n:n + 1, :] = packed(blocks, TY - 1)
        ys_n[n:n + 1, :] = packed(blocks, 0)
    for c in range(3):
        blocks = [vel_n[c, rows(x), :] for x in range(TX)]
        ys_p[5 + c:6 + c, :] = packed(blocks, TY - 1)
        ys_n[5 + c:6 + c, :] = packed(blocks, 0)
    for n in range(5):
        ys_p[8 + n:9 + n, :] = packed([post_v[YP[n], rows(x), :] for x in range(TX)], TY - 1)
        ys_n[8 + n:9 + n, :] = packed([post_v[YN[n], rows(x), :] for x in range(TX)], 0)
    for n in range(5):
        xs_p[n] = post_v[XP[n], rows(TX - 1), :]
        xs_n[n] = post_v[XN[n], rows(0), :]
        xs_p[5 + n] = g_v[n, rows(TX - 1), :]
        xs_n[5 + n] = g_v[n, rows(0), :]
    for c in range(3):
        xs_p[10 + c] = vel_n[c, rows(TX - 1), :]

    pl.semaphore_wait(barrier, len(PEERS))
    send_y = []
    for n, t in reversed(list(enumerate(HOPS))):
        send_y.append(remote(ys_p, yr_p.at[n], yp_sem, n, t, 1))
        send_y.append(remote(ys_n, yr_n.at[n], yn_sem, n, t, -1))
    send_vel = remote(vel_n, vel_f, v_sem, 0, -1, 0)
    send_x = [remote(xs_p, xr_m, x_sem, 0, 1, 0), remote(xs_n, xr_p, x_sem, 1, -1, 0),
              remote(g_v.at[:, 2 * CELLS - NZ:, :], gr_2, g_sem, 1, 2, 0),
              remote(g_v.at[:, CELLS:, :], gr_1, g_sem, 0, 1, 0)]
    for copy in send_y + [send_vel] + send_x:
        copy.start()

    def interpolated(table, b):
        spot, row = place(b)
        frac = frac_v[pl.ds(b * 8, 8), :]
        rest = 1.0 - frac
        found = [jnp.zeros((8, MK), F32) for _ in range(3)]
        for r in range(CELLS):
            weight = jnp.where(row == r, rest, jnp.where(row == r - 1, frac, 0.0))
            for c in range(3):
                line = jnp.broadcast_to(table[c, r:r + 1, :], (8, TY))
                found[c] = found[c] + weight * jnp.take_along_axis(line, spot, axis=1)
        return found

    def near_step(b, carry):
        for c, found in enumerate(interpolated(vel_n, b)):
            mf_v[c, pl.ds(b * 8, 8), :] = STIFFNESS * (blade_v[c, pl.ds(b * 8, 8), :] - found)
        return carry

    def far_step(b, carry):
        far = side_v[pl.ds(b * 8, 8), :] == 1
        for c, found in enumerate(interpolated(vel_f, b)):
            force = STIFFNESS * (blade_v[c, pl.ds(b * 8, 8), :] - found)
            mf_v[c, pl.ds(b * 8, 8), :] = jnp.where(far, force, mf_v[c, pl.ds(b * 8, 8), :])
        return carry

    lax.fori_loop(0, BL // 8, near_step, 0, unroll=4)
    send_vel.wait()
    lax.fori_loop(0, BL // 8, far_step, 0, unroll=4)
    for copy in send_x:
        copy.wait()

    force = {}
    for x in range(-1, TX + 1):
        if x == -1:
            fields = [xr_m[5 + n] + gr_2[n] for n in range(5)]
            vel = [xr_m[10 + c] for c in range(3)]
        elif x == TX:
            fields = [g_v[n, rows(TX), :] + xr_p[5 + n] for n in range(5)]
            vel = [vel_f[c, rows(0), :] for c in range(3)]
        else:
            fields = [g_v[n, rows(x), :] + gr_1[n, rows(x), :] for n in range(5)]
            vel = [vel_n[c, rows(x), :] for c in range(3)]
        force[x] = force_of(fields, vel, 0)

    _, plane = lanes_and_planes()

    def post_at(i, x):
        if x == -1:
            value = xr_m[XP.index(i)]
        elif x == TX:
            value = xr_p[XN.index(i)]
        else:
            value = post_v[i, rows(x), :]
        push = pushed(i, force[x])
        return value if push is None else value + push

    def moved(i, x):
        value = post_at(i, x)
        cy = VELOCITIES[i][1]
        return value if cy == 0 else pltpu.roll(value, cy % TY, 1)

    for x in range(TX):
        for i in range(19):
            cx, _, cz = VELOCITIES[i]
            value = moved(i, x - cx)
            if cz == 1:
                value = jnp.where(plane == 0, post_at(opposite_of(i), x), pltpu.roll(value, 1, 0))
            elif cz == -1:
                value = jnp.where(plane == NZ - 1, moved(mirror_of(i), x - cx), pltpu.roll(value, NZ - 1, 0))
            new_v[i, planes(x), :] = value

    for copy in send_y:
        copy.wait()


def finish(mid, mf, yr_p, yr_n, new_h, mf_h, new_v, sem):
    straight = [i for i in range(19) if VELOCITIES[i][1] == 0]
    copies = [pltpu.make_async_copy(mid.at[i], new_h.at[i], sem.at[i]) for i in straight]
    copies.append(pltpu.make_async_copy(mf, mf_h, sem.at[19]))
    for copy in copies:
        copy.start()
    lane, plane = lanes_and_planes()

    def edge(ref, group):
        total = None
        for n, t in enumerate(HOPS):
            part = pltpu.roll(ref[n], (NZ - NZ * TX * t) % TY, 1)
            total = part if total is None else total + part
        line = [total[n:n + 1, :] for n in range(13)]
        force = force_of(line[:5], line[5:8], 1)
        return {i: line[8 + n] + pushed(i, force) for n, i in enumerate(group)}

    edges = edge(yr_p, YP)
    edges.update(edge(yr_n, YN))

    def column(i, x):
        spot = lane == plane + (x + 1) * NZ
        return jnp.broadcast_to(
            jnp.sum(jnp.where(spot, jnp.broadcast_to(edges[i], (NZ, TY)), 0.0), axis=1, keepdims=True), (NZ, TY))

    for i in YP + YN:
        cx, cy, cz = VELOCITIES[i]
        here = lane == (0 if cy == 1 else TY - 1)
        for x in range(TX):
            value = column(i, x - cx)
            where = here
            if cz == 1:
                value = pltpu.roll(value, 1, 0)
                where = jnp.logical_and(here, plane > 0)
            elif cz == -1:
                value = jnp.where(plane == NZ - 1, column(mirror_of(i), x - cx), pltpu.roll(value, NZ - 1, 0))
            new_v[i, planes(x), :] = jnp.where(where, value, mid[i, planes(x), :])
        copy = pltpu.make_async_copy(new_v.at[i], new_h.at[i], sem.at[i])
        copy.start()
        copies.append(copy)
    for copy in copies:
        copy.wait()


def local(dist, marker_cell, marker_side, marker_frac, blade_vel):
    hbm = pl.BlockSpec(memory_space=pltpu.HBM)
    vmem = pl.BlockSpec(memory_space=pltpu.VMEM)
    cells = pltpu.VMEM((19, CELLS, TY), F32)
    field = pltpu.VMEM((3, CELLS, TY), F32)
    edge = pltpu.VMEM((16, TY), F32)
    dma = pltpu.SemaphoreType.DMA
    shape = jax.ShapeDtypeStruct
    given = [pltpu.with_memory_space_constraint(a, pltpu.HBM) for a in (
        dist.reshape(19, CELLS, TY), marker_cell, marker_side, marker_frac, blade_vel)]
    mid, mf, yr_p, yr_n = pl.pallas_call(
        exchange,
        out_shape=(shape((19, CELLS, TY), F32), shape((3, BL, MK), F32),
                   shape((4, 16, TY), F32), shape((4, 16, TY), F32)),
        in_specs=[hbm] * 5,
        out_specs=(vmem,) * 4,
        scratch_shapes=[
            cells, pltpu.VMEM((BL, MK), jnp.int32), pltpu.VMEM((BL, MK), jnp.int32), pltpu.VMEM((BL, MK), F32),
            pltpu.VMEM((3, BL, MK), F32),
            field, field, cells, pltpu.VMEM((13, NZ, TY), F32), pltpu.VMEM((10, NZ, TY), F32),
            pltpu.VMEM((13, NZ, TY), F32), pltpu.VMEM((10, NZ, TY), F32),
            pltpu.VMEM((5, 2 * CELLS, TY), F32), pltpu.VMEM((5, CELLS, TY), F32), pltpu.VMEM((5, NZ, TY), F32),
            edge, edge,
            dma((5,)), dma((2, 1)), dma((2, 2)), dma((2, 2)), dma((2, 4)), dma((2, 4)),
        ],
        compiler_params=pltpu.CompilerParams(collective_id=0, has_side_effects=True, vmem_limit_bytes=32 * 2**20),
        name="exchange",
    )(*given)
    new, force = pl.pallas_call(
        finish,
        out_shape=(shape((19, CELLS, TY), F32), shape((3, BL, MK), F32)),
        in_specs=[vmem] * 4,
        out_specs=(hbm, hbm),
        scratch_shapes=[cells, dma((20,))],
        compiler_params=pltpu.CompilerParams(vmem_limit_bytes=16 * 2**20),
        name="finish",
    )(mid, mf, yr_p, yr_n)
    return new.reshape(dist.shape), force


def solution(mesh):
    return jax.shard_map(
        local,
        mesh=mesh,
        in_specs=(
            P(None, None, "gx", "gy"),
            P(("gx", "gy"), None),
            P(("gx", "gy"), None),
            P(("gx", "gy"), None),
            P(None, ("gx", "gy"), None),
        ),
        out_specs=(P(None, None, "gx", "gy"), P(None, ("gx", "gy"), None)),
        check_vma=False,
    )
```

time: 27.2 us -> 21.6 us (0.79)
  Pallas kernels: 26.4 us -> 20.8 us
    pallas_call x1, Pallas kernels: 25.4 us -> 19.8 us  [local(): pl.pallas_call(exchange, out_shape=(shape((19, CELLS, TY), F32), shape((3...]
where the time goes in v3:
time: 21.6 us; the launch traced here: 21.5 us
  Pallas kernels  20.8 us (96%)
  between operations  0.64 us (3%)
    pallas_call x1, Pallas kernels, local(): pl.pallas_call(exchange, out_shape=(shape((19, CELLS, TY), F32), shape((3...  19.8 us
    pallas_call x1, Pallas kernels, local(): pl.pallas_call(finish, out_shape=(shape((19, CELLS, TY), F32), shape((3,...  1.07 us

profile of v3, /device:TPU:1, one launch (start us, length us, event | category | flops | bytes accessed | tf_op | source)
XLA Modules:
  0.0 21.5 jit_solution(453302391635484258)
XLA Ops:
  0.6 19.8 %exchange.1 = (f32[19,32,128]{2,1,0:T(8,128)S(1)}, f32[3,64,128]{2,1,0:T(8,128)S(1)}, f32[4,16,128]{2,1,0:T(8,128)S(1)}, f32[4,16,128]{2,1,0:T(8,128)S(1)}) custom-call(f32[19,32,128]{2,1,0:T(8,128)} %bitcast.2, s32[64,128]{1,0:T(8,128)} %cell_h.1, s32[64,128]{1,0:T(8,128)} %side_h.1, f32[64,128]{1,0:T(8,128)} %frac_h.1, f32[3,64,128]{2,1,0:T(8,128)} %blade_h.1), custom_call_target="tpu_custom_call" | custom-call | tf_op jit(solution)/shard_map/exchange/pallas_call | solution.py:379
  20.4 1.1 %finish.1 = (f32[19,32,128]{2,1,0:T(8,128)}, f32[3,64,128]{2,1,0:T(8,128)}) custom-call(f32[19,32,128]{2,1,0:T(8,128)S(1)} %get-tuple-element.8.mid, f32[3,64,128]{2,1,0:T(8,128)S(1)} %get-tuple-element.9.mf, f32[4,16,128]{2,1,0:T(8,128)S(1)} %get-tuple-element.10.yr_p, f32[4,16,128]{2,1,0:T(8,128)S(1)} %get-tuple-element.11.yr_n), custom_call_target="tpu_custom_call" | custom-call | tf_op jit(solution)/shard_map/finish/pallas_call | solution.py:397

commit v4 on v3

--- a/solution.py
+++ b/solution.py
@@ -113,12 +113,14 @@
     return (lax.broadcasted_iota(jnp.int32, (NZ, TY), 1), lax.broadcasted_iota(jnp.int32, (NZ, TY), 0))
 
 
-def packed(blocks, column):
+def packed(groups, column):
     lane, plane = lanes_and_planes()
     total = None
-    for n, block in enumerate(blocks):
-        part = jnp.where(lane == plane + n * NZ, jnp.broadcast_to(block[:, column:column + 1], (NZ, TY)), 0.0)
-        total = part if total is None else total + part
+    for g, blocks in enumerate(groups):
+        for n, block in enumerate(blocks):
+            part = jnp.where(lane == plane + (g * TX + n) * NZ,
+                             jnp.broadcast_to(block[:, column:column + 1], (NZ, TY)), 0.0)
+            total = part if total is None else total + part
     return jnp.sum(total, axis=0, keepdims=True)
 
 
@@ -135,7 +137,7 @@
 def exchange(dist_h, cell_h, side_h, frac_h, blade_h, new_v, mf_v, yr_p, yr_n,
              dist_v, cell_v, side_v, frac_v, blade_v,
              vel_n, vel_f, post_v, xs_p, xs_n, xr_m, xr_p,
-             g_v, gr_1, gr_2, ys_p, ys_n,
+             g_v, gf_v, gr_1, gr_2, ys_p, ys_n,
              in_sem, v_sem, x_sem, g_sem, yp_sem, yn_sem):
     n_gx, n_gy = lax.axis_size("gx"), lax.axis_size("gy")
     gx, gy = lax.axis_index("gx"), lax.axis_index("gy")
@@ -155,17 +157,8 @@
         ((cell_h, cell_v), (side_h, side_v), (frac_h, frac_v), (blade_h, blade_v), (dist_h, dist_v)))]
     for load in loads:
         load.start()
-    for load in loads:
+    for load in loads[:4]:
         load.wait()
-
-    for x in range(TX):
-        values = [dist_v[i, planes(x), :] for i in range(19)]
-        _, _, rho, jx, jy, jz = momentum_of(values)
-        inv = 1.0 / rho
-        for c, j in enumerate((jx, jy, jz)):
-            vel_n[c, rows(x), :] = j * inv
-        for i, post in enumerate(collided(values)):
-            post_v[i, rows(x), :] = post
 
     spots = lax.broadcasted_iota(jnp.int32, (2 * TY, MK), 0).astype(F32).astype(BF16)
     lines = lax.broadcasted_iota(jnp.int32, (CELLS, MK), 0).astype(F32).astype(BF16)
@@ -212,40 +205,59 @@
     total = lax.fori_loop(0, BL // 8, scatter_step, jnp.zeros((10 * CELLS, 2 * TY), F32), unroll=8)
     for n in range(5):
         both = total[2 * n * CELLS:(2 * n + 1) * CELLS] + total[(2 * n + 1) * CELLS:(2 * n + 2) * CELLS]
-        g_v[n, 0:CELLS, :] = both[:, :TY]
-        g_v[n, CELLS:2 * CELLS, :] = both[:, TY:]
-
-    ys_p[...] = jnp.zeros_like(ys_p)
-    ys_n[...] = jnp.zeros_like(ys_n)
-    for n in range(5):
-        blocks = [g_v[n, rows(x), :] for x in range(2 * TX)]
-        ys_p[n:n + 1, :] = packed(blocks, TY - 1)
-        ys_n[n:n + 1, :] = packed(blocks, 0)
-    for c in range(3):
-        blocks = [vel_n[c, rows(x), :] for x in range(TX)]
-        ys_p[5 + c:6 + c, :] = packed(blocks, TY - 1)
-        ys_n[5 + c:6 + c, :] = packed(blocks, 0)
-    for n in range(5):
-        ys_p[8 + n:9 + n, :] = packed([post_v[YP[n], rows(x), :] for x in range(TX)], TY - 1)
-        ys_n[8 + n:9 + n, :] = packed([post_v[YN[n], rows(x), :] for x in range(TX)], 0)
-    for n in range(5):
-        xs_p[n] = post_v[XP[n], rows(TX - 1), :]
-        xs_n[n] = post_v[XN[n], rows(0), :]
-        xs_p[5 + n] = g_v[n, rows(TX - 1), :]
-        xs_n[5 + n] = g_v[n, rows(0), :]
-    for c in range(3):
-        xs_p[10 + c] = vel_n[c, rows(TX - 1), :]
-
+        g_v[n] = both[:, :TY]
+        gf_v[n] = both[:, TY:]
+
+    sides = ((ys_p, yr_p, yp_sem, YP, TY - 1, 1), (ys_n, yr_n, yn_sem, YN, 0, -1))
+    fields = [[gf_v[n, rows(x), :] for x in range(TX)] for n in range(5)]
+    for ref, _, _, _, column, _ in sides:
+        ref[2:3, :] = packed(fields[:4], column)
+        ref[3:4, :] = packed(fields[4:], column)
     pl.semaphore_wait(barrier, len(PEERS))
     send_y = []
-    for n, t in reversed(list(enumerate(HOPS))):
-        send_y.append(remote(ys_p, yr_p.at[n], yp_sem, n, t, 1))
-        send_y.append(remote(ys_n, yr_n.at[n], yn_sem, n, t, -1))
+    for ref, landing, sems, _, _, s in sides:
+        send_y.append(remote(ref.at[2:4], landing.at[3, 2:4], sems, 3, 2, s))
+    for copy in send_y:
+        copy.start()
+
+    loads[4].wait()
+    for x in range(TX):
+        values = [dist_v[i, planes(x), :] for i in range(19)]
+        _, _, rho, jx, jy, jz = momentum_of(values)
+        inv = 1.0 / rho
+        for c, j in enumerate((jx, jy, jz)):
+            vel_n[c, rows(x), :] = j * inv
+        for i, post in enumerate(collided(values)):
+            post_v[i, rows(x), :] = post
+
+    for x in range(TX):
+        own = force_of([g_v[n, rows(x), :] for n in range(5)], [vel_n[c, rows(x), :] for c in range(3)], 0)
+        for i in range(1, 19):
+            post_v[i, rows(x), :] = post_v[i, rows(x), :] + pushed(i, own)
+
+    for ref, _, _, group, column, _ in sides:
+        parts = ([[post_v[i, rows(x), :] for x in range(TX)] for i in group]
+                 + [[vel_n[c, rows(x), :] for x in range(TX)] for c in range(3)])
+        ref[0:1, :] = packed(parts[:4], column)
+        ref[1:2, :] = packed(parts[4:], column)
+    for ref, group, x in ((xs_p, XP, TX - 1), (xs_n, XN, 0)):
+        for n, i in enumerate(group):
+            ref[n] = post_v[i, rows(x), :]
+    for c in range(3):
+        xs_p[5 + c] = vel_n[c, rows(TX - 1), :]
+        xs_n[5 + c] = vel_n[c, rows(0), :]
+
+    later = []
+    for n, t in ((2, 1), (1, 0), (0, -1)):
+        part = slice(0, 2) if t == -1 else slice(0, 4)
+        for ref, landing, sems, _, _, s in sides:
+            later.append(remote(ref.at[part], landing.at[n, part], sems, n, t, s))
     send_vel = remote(vel_n, vel_f, v_sem, 0, -1, 0)
-    send_x = [remote(xs_p, xr_m, x_sem, 0, 1, 0), remote(xs_n, xr_p, x_sem, 1, -1, 0),
-              remote(g_v.at[:, 2 * CELLS - NZ:, :], gr_2, g_sem, 1, 2, 0),
-              remote(g_v.at[:, CELLS:, :], gr_1, g_sem, 0, 1, 0)]
-    for copy in send_y + [send_vel] + send_x:
+    send_x = [remote(gf_v, gr_1, g_sem, 0, 1, 0),
+              remote(xs_p, xr_m, x_sem, 0, 1, 0),
+              remote(gf_v.at[:, CELLS - NZ:, :], gr_2, g_sem, 1, 2, 0),
+              remote(xs_n, xr_p, x_sem, 1, -1, 0)]
+    for copy in later + [send_vel, send_x[1], send_x[3], send_x[2], send_x[0]]:
         copy.start()
 
     def interpolated(table, b):
@@ -281,13 +293,13 @@
     force = {}
     for x in range(-1, TX + 1):
         if x == -1:
-            fields = [xr_m[5 + n] + gr_2[n] for n in range(5)]
-            vel = [xr_m[10 + c] for c in range(3)]
+            fields = [gr_2[n] for n in range(5)]
+            vel = [xr_m[5 + c] for c in range(3)]
         elif x == TX:
-            fields = [g_v[n, rows(TX), :] + xr_p[5 + n] for n in range(5)]
-            vel = [vel_f[c, rows(0), :] for c in range(3)]
+            fields = [gf_v[n, rows(0), :] for n in range(5)]
+            vel = [xr_p[5 + c] for c in range(3)]
         else:
-            fields = [g_v[n, rows(x), :] + gr_1[n, rows(x), :] for n in range(5)]
+            fields = [gr_1[n, rows(x), :] for n in range(5)]
             vel = [vel_n[c, rows(x), :] for c in range(3)]
         force[x] = force_of(fields, vel, 0)
 
@@ -318,8 +330,10 @@
                 value = jnp.where(plane == NZ - 1, moved(mirror_of(i), x - cx), pltpu.roll(value, NZ - 1, 0))
             new_v[i, planes(x), :] = value
 
-    for copy in send_y:
-        copy.wait()
+    for copy in send_y + later:
+        copy.wait_send()
+    for copy in later + send_y:
+        copy.wait_recv()
 
 
 def finish(mid, mf, yr_p, yr_n, new_h, mf_h, new_v, sem):
@@ -330,17 +344,25 @@
         copy.start()
     lane, plane = lanes_and_planes()
 
-    def edge(ref, group):
-        total = None
-        for n, t in enumerate(HOPS):
-            part = pltpu.roll(ref[n], (NZ - NZ * TX * t) % TY, 1)
-            total = part if total is None else total + part
-        line = [total[n:n + 1, :] for n in range(13)]
-        force = force_of(line[:5], line[5:8], 1)
-        return {i: line[8 + n] + pushed(i, force) for n, i in enumerate(group)}
-
-    edges = edge(yr_p, YP)
-    edges.update(edge(yr_n, YN))
+    row = lax.broadcasted_iota(jnp.int32, (4, TY), 0)
+
+    def source(first, second):
+        return jnp.concatenate([jnp.where(row < 2, ref[first], ref[second]) for ref in (yr_p, yr_n)], axis=0)
+
+    before, own, after = source(2, 3), source(1, 2), source(0, 1)
+    lines = []
+    for g in range(4):
+        turn = TY - 4 * NZ * g
+        line = jnp.where(lane < NZ, pltpu.roll(before, (turn - 3 * NZ) % TY, 1),
+                         jnp.where(lane < 5 * NZ, pltpu.roll(own, (turn + NZ) % TY, 1),
+                                   pltpu.roll(after, (turn + 5 * NZ) % TY, 1)))
+        lines.append(jnp.where(lane < 6 * NZ, line, 0.0))
+    edges = {}
+    for n, group in enumerate((YP, YN)):
+        line = [lines[q % 4][4 * n + q // 4:4 * n + q // 4 + 1, :] for q in range(13)]
+        force = force_of(line[8:], line[5:8], 1)
+        for q, i in enumerate(group):
+            edges[i] = line[q] + pushed(i, force)
 
     def column(i, x):
         spot = lane == plane + (x + 1) * NZ
@@ -371,7 +393,7 @@
     vmem = pl.BlockSpec(memory_space=pltpu.VMEM)
     cells = pltpu.VMEM((19, CELLS, TY), F32)
     field = pltpu.VMEM((3, CELLS, TY), F32)
-    edge = pltpu.VMEM((16, TY), F32)
+    edge = pltpu.VMEM((4, TY), F32)
     dma = pltpu.SemaphoreType.DMA
     shape = jax.ShapeDtypeStruct
     given = [pltpu.with_memory_space_constraint(a, pltpu.HBM) for a in (
@@ -379,15 +401,15 @@
     mid, mf, yr_p, yr_n = pl.pallas_call(
         exchange,
         out_shape=(shape((19, CELLS, TY), F32), shape((3, BL, MK), F32),
-                   shape((4, 16, TY), F32), shape((4, 16, TY), F32)),
+                   shape((4, 4, TY), F32), shape((4, 4, TY), F32)),
         in_specs=[hbm] * 5,
         out_specs=(vmem,) * 4,
         scratch_shapes=[
             cells, pltpu.VMEM((BL, MK), jnp.int32), pltpu.VMEM((BL, MK), jnp.int32), pltpu.VMEM((BL, MK), F32),
             pltpu.VMEM((3, BL, MK), F32),
-            field, field, cells, pltpu.VMEM((13, NZ, TY), F32), pltpu.VMEM((10, NZ, TY), F32),
-            pltpu.VMEM((13, NZ, TY), F32), pltpu.VMEM((10, NZ, TY), F32),
-            pltpu.VMEM((5, 2 * CELLS, TY), F32), pltpu.VMEM((5, CELLS, TY), F32), pltpu.VMEM((5, NZ, TY), F32),
+            field, field, cells, pltpu.VMEM((8, NZ, TY), F32), pltpu.VMEM((8, NZ, TY), F32),
+            pltpu.VMEM((8, NZ, TY), F32), pltpu.VMEM((8, NZ, TY), F32),
+            pltpu.VMEM((5, CELLS, TY), F32), pltpu.VMEM((5, CELLS, TY), F32), pltpu.VMEM((5, CELLS, TY), F32), pltpu.VMEM((5, NZ, TY), F32),
             edge, edge,
             dma((5,)), dma((2, 1)), dma((2, 2)), dma((2, 2)), dma((2, 4)), dma((2, 4)),
         ],

time: 21.6 us -> 21.2 us (0.981)
  Pallas kernels: 20.8 us -> 20.4 us
    pallas_call x1, Pallas kernels: 19.8 us -> 19.3 us  [local(): pl.pallas_call(exchange, out_shape=(shape((19, CELLS, TY), F32), shape((3...]
where the time goes in v4:
time: 21.2 us; the launch traced here: 21 us
  Pallas kernels  20.4 us (96%)
  between operations  0.64 us (3%)
    pallas_call x1, Pallas kernels, local(): pl.pallas_call(exchange, out_shape=(shape((19, CELLS, TY), F32), shape((3...  19.3 us
    pallas_call x1, Pallas kernels, local(): pl.pallas_call(finish, out_shape=(shape((19, CELLS, TY), F32), shape((3,...  1.08 us

profile of v4, /device:TPU:1, one launch (start us, length us, event | category | flops | bytes accessed | tf_op | source)
XLA Modules:
  0.0 21.0 jit_solution(8566118387803232685)
XLA Ops:
  0.6 19.3 %exchange.1 = (f32[19,32,128]{2,1,0:T(8,128)S(1)}, f32[3,64,128]{2,1,0:T(8,128)S(1)}, f32[4,4,128]{2,1,0:T(4,128)S(1)}, f32[4,4,128]{2,1,0:T(4,128)S(1)}) custom-call(f32[19,32,128]{2,1,0:T(8,128)} %bitcast.2, s32[64,128]{1,0:T(8,128)} %cell_h.1, s32[64,128]{1,0:T(8,128)} %side_h.1, f32[64,128]{1,0:T(8,128)} %frac_h.1, f32[3,64,128]{2,1,0:T(8,128)} %blade_h.1), custom_call_target="tpu_custom_call" | custom-call | tf_op jit(solution)/shard_map/exchange/pallas_call | solution.py:401
  20.0 1.1 %finish.1 = (f32[19,32,128]{2,1,0:T(8,128)}, f32[3,64,128]{2,1,0:T(8,128)}) custom-call(f32[19,32,128]{2,1,0:T(8,128)S(1)} %get-tuple-element.8.mid, f32[3,64,128]{2,1,0:T(8,128)S(1)} %get-tuple-element.9.mf, f32[4,4,128]{2,1,0:T(4,128)S(1)} %get-tuple-element.10.yr_p, f32[4,4,128]{2,1,0:T(4,128)S(1)} %get-tuple-element.11.yr_n), custom_call_target="tpu_custom_call" | custom-call | tf_op jit(solution)/shard_map/finish/pallas_call | solution.py:419

commit v5 on v4

--- a/solution.py
+++ b/solution.py
@@ -336,12 +336,11 @@
         copy.wait_recv()
 
 
-def finish(mid, mf, yr_p, yr_n, new_h, mf_h, new_v, sem):
-    straight = [i for i in range(19) if VELOCITIES[i][1] == 0]
-    copies = [pltpu.make_async_copy(mid.at[i], new_h.at[i], sem.at[i]) for i in straight]
-    copies.append(pltpu.make_async_copy(mf, mf_h, sem.at[19]))
-    for copy in copies:
-        copy.start()
+def finish(mid, mf, yr_p, yr_n, new_v, mf_v):
+    for i in range(19):
+        if VELOCITIES[i][1] == 0:
+            new_v[i] = mid[i]
+    mf_v[...] = mf[...]
     lane, plane = lanes_and_planes()
 
     row = lax.broadcasted_iota(jnp.int32, (4, TY), 0)
@@ -364,10 +363,14 @@
         for q, i in enumerate(group):
             edges[i] = line[q] + pushed(i, force)
 
+    columns = {}
+
     def column(i, x):
-        spot = lane == plane + (x + 1) * NZ
-        return jnp.broadcast_to(
-            jnp.sum(jnp.where(spot, jnp.broadcast_to(edges[i], (NZ, TY)), 0.0), axis=1, keepdims=True), (NZ, TY))
+        if (i, x) not in columns:
+            spot = lane == plane + (x + 1) * NZ
+            column = jnp.sum(jnp.where(spot, jnp.broadcast_to(edges[i], (NZ, TY)), 0.0), axis=1, keepdims=True)
+            columns[i, x] = jnp.broadcast_to(column, (NZ, TY))
+        return columns[i, x]
 
     for i in YP + YN:
         cx, cy, cz = VELOCITIES[i]
@@ -381,11 +384,6 @@
             elif cz == -1:
                 value = jnp.where(plane == NZ - 1, column(mirror_of(i), x - cx), pltpu.roll(value, NZ - 1, 0))
             new_v[i, planes(x), :] = jnp.where(where, value, mid[i, planes(x), :])
-        copy = pltpu.make_async_copy(new_v.at[i], new_h.at[i], sem.at[i])
-        copy.start()
-        copies.append(copy)
-    for copy in copies:
-        copy.wait()
 
 
 def local(dist, marker_cell, marker_side, marker_frac, blade_vel):
@@ -420,8 +418,7 @@
         finish,
         out_shape=(shape((19, CELLS, TY), F32), shape((3, BL, MK), F32)),
         in_specs=[vmem] * 4,
-        out_specs=(hbm, hbm),
-        scratch_shapes=[cells, dma((20,))],
+        out_specs=(vmem, vmem),
         compiler_params=pltpu.CompilerParams(vmem_limit_bytes=16 * 2**20),
         name="finish",
     )(mid, mf, yr_p, yr_n)

time: 21.2 us -> 21.1 us (level)
  no operation moved by 1% of the time
where the time goes in v5:
time: 21.1 us; the launch traced here: 21 us
  Pallas kernels  20.3 us (96%)
  between operations  0.64 us (3%)
    pallas_call x1, Pallas kernels, local(): pl.pallas_call(exchange, out_shape=(shape((19, CELLS, TY), F32), shape((3...  19.3 us
    pallas_call x1, Pallas kernels, local(): pl.pallas_call(finish, out_shape=(shape((19, CELLS, TY), F32), shape((3,...  1 us

profile of v5, /device:TPU:1, one launch (start us, length us, event | category | flops | bytes accessed | tf_op | source)
XLA Modules:
  0.0 21.0 jit_solution(15405322560810398171)
XLA Ops:
  0.6 19.3 %exchange.1 = (f32[19,32,128]{2,1,0:T(8,128)S(1)}, f32[3,64,128]{2,1,0:T(8,128)S(1)}, f32[4,4,128]{2,1,0:T(4,128)S(1)}, f32[4,4,128]{2,1,0:T(4,128)S(1)}) custom-call(f32[19,32,128]{2,1,0:T(8,128)} %bitcast.2, s32[64,128]{1,0:T(8,128)} %cell_h.1, s32[64,128]{1,0:T(8,128)} %side_h.1, f32[64,128]{1,0:T(8,128)} %frac_h.1, f32[3,64,128]{2,1,0:T(8,128)} %blade_h.1), custom_call_target="tpu_custom_call" | custom-call | tf_op jit(solution)/shard_map/exchange/pallas_call | solution.py:399
  20.0 1.0 %finish.1 = (f32[19,32,128]{2,1,0:T(8,128)}, f32[3,64,128]{2,1,0:T(8,128)}) custom-call(f32[19,32,128]{2,1,0:T(8,128)S(1)} %get-tuple-element.8.mid, f32[3,64,128]{2,1,0:T(8,128)S(1)} %get-tuple-element.9.mf, f32[4,4,128]{2,1,0:T(4,128)S(1)} %get-tuple-element.10.yr_p, f32[4,4,128]{2,1,0:T(4,128)S(1)} %get-tuple-element.11.yr_n), custom_call_target="tpu_custom_call" | custom-call | tf_op jit(solution)/shard_map/finish/pallas_call | solution.py:417

commit v6 on v5

--- a/solution.py
+++ b/solution.py
@@ -248,7 +248,7 @@
         xs_n[5 + c] = vel_n[c, rows(0), :]
 
     later = []
-    for n, t in ((2, 1), (1, 0), (0, -1)):
+    for n, t in ((0, -1), (2, 1), (1, 0)):
         part = slice(0, 2) if t == -1 else slice(0, 4)
         for ref, landing, sems, _, _, s in sides:
             later.append(remote(ref.at[part], landing.at[n, part], sems, n, t, s))

time: 21.1 us -> 21.1 us (level)
  no operation moved by 1% of the time
where the time goes in v6:
time: 21.1 us; the launch traced here: 21 us
  Pallas kernels  20.3 us (96%)
  between operations  0.64 us (3%)
    pallas_call x1, Pallas kernels, local(): pl.pallas_call(exchange, out_shape=(shape((19, CELLS, TY), F32), shape((3...  19.3 us
    pallas_call x1, Pallas kernels, local(): pl.pallas_call(finish, out_shape=(shape((19, CELLS, TY), F32), shape((3,...  1 us

profile of v6, /device:TPU:1, one launch (start us, length us, event | category | flops | bytes accessed | tf_op | source)
XLA Modules:
  0.0 21.0 jit_solution(4497618043091205996)
XLA Ops:
  0.6 19.3 %exchange.1 = (f32[19,32,128]{2,1,0:T(8,128)S(1)}, f32[3,64,128]{2,1,0:T(8,128)S(1)}, f32[4,4,128]{2,1,0:T(4,128)S(1)}, f32[4,4,128]{2,1,0:T(4,128)S(1)}) custom-call(f32[19,32,128]{2,1,0:T(8,128)} %bitcast.2, s32[64,128]{1,0:T(8,128)} %cell_h.1, s32[64,128]{1,0:T(8,128)} %side_h.1, f32[64,128]{1,0:T(8,128)} %frac_h.1, f32[3,64,128]{2,1,0:T(8,128)} %blade_h.1), custom_call_target="tpu_custom_call" | custom-call | tf_op jit(solution)/shard_map/exchange/pallas_call | solution.py:399
  20.0 1.0 %finish.1 = (f32[19,32,128]{2,1,0:T(8,128)}, f32[3,64,128]{2,1,0:T(8,128)}) custom-call(f32[19,32,128]{2,1,0:T(8,128)S(1)} %get-tuple-element.8.mid, f32[3,64,128]{2,1,0:T(8,128)S(1)} %get-tuple-element.9.mf, f32[4,4,128]{2,1,0:T(4,128)S(1)} %get-tuple-element.10.yr_p, f32[4,4,128]{2,1,0:T(4,128)S(1)} %get-tuple-element.11.yr_n), custom_call_target="tpu_custom_call" | custom-call | tf_op jit(solution)/shard_map/finish/pallas_call | solution.py:417
